TPU v7x, 128 devices: a whole 4x4x4 slice. The times are simulated.
128 devices in a mesh: expert: 16 (over z, x), tensor: 8 (over y, core).
Axes of the slice: x: 4, y: 4, z: 4, core: 2. Of those that a mesh axis runs over, the one named last changes fastest.
Arguments:
- tokens: bfloat16 [2048, 4096], P('expert'), may hold values from -6 to 6
- cotangent: bfloat16 [2048, 4096], P('expert'), may hold values from -6 to 6
- expert_ids: int32 [2048, 8], P('expert'), may hold values from 0 to 127, all different within a row; in each aligned block of 128 rows (0 to 127, 128 to 255, ...) at most 9 rows name the same one
- gate_probs: float32 [2048, 8], P('expert'), may hold values from 0.05 to 1
- w_gate: bfloat16 [128, 896, 4096], P('expert', 'tensor'), may hold values from -0.09375 to 0.09375
- w_up: bfloat16 [128, 896, 4096], P('expert', 'tensor'), may hold values from -0.09375 to 0.09375
- w_down: bfloat16 [128, 896, 4096], P('expert', 'tensor'), may hold values from -0.1875 to 0.1875
Outputs:
- mixed: bfloat16 [2048, 4096], P('expert')
- grad_tokens: bfloat16 [2048, 4096], P('expert')
Inputs may be any that keep to these rules, and one draw needn't show every extreme that they name: `expert_ids`: each token names 8 different experts; the 128 tokens of one index of the expert axis name one expert at most 9 times, a bound that some block reaches.
All inputs are finite; a program needn't handle non-finite values.
Results may differ from a plain program's by a relative error of at most 0.017.
Values may be sent and summed in bfloat16 or wider, within the bound.
A program may use at most 192 MiB of HBM per device.

v0:
```python
import jax
import jax.numpy as jnp
from jax import lax
from jax.sharding import PartitionSpec as P


def expert_work(segment, w_gate, w_up, w_down, features):
    token_part = segment[..., :features]
    scaled_part = segment[..., features:]
    pre_gate = jnp.einsum("sicd,ihd->sich", token_part, w_gate, preferred_element_type=jnp.float32)
    up_value = jnp.einsum("sicd,ihd->sich", token_part, w_up, preferred_element_type=jnp.float32)
    sigmoid_gate = jax.nn.sigmoid(pre_gate)
    activated = pre_gate * sigmoid_gate
    hidden = (activated * up_value).astype(jnp.bfloat16)
    output_rows = jnp.einsum("sich,ihd->sicd", hidden, w_down, preferred_element_type=jnp.float32)
    grad_hidden = jnp.einsum(
        "sicd,ihd->sich", scaled_part, w_down, preferred_element_type=jnp.float32
    )
    grad_gate = (
        grad_hidden * up_value * sigmoid_gate * (1.0 + pre_gate * (1.0 - sigmoid_gate))
    ).astype(jnp.bfloat16)
    grad_up = (grad_hidden * activated).astype(jnp.bfloat16)
    grad_rows = jnp.einsum("sich,ihd->sicd", grad_gate, w_gate, preferred_element_type=jnp.float32)
    grad_rows = grad_rows + jnp.einsum(
        "sich,ihd->sicd", grad_up, w_up, preferred_element_type=jnp.float32
    )
    return jnp.concatenate([output_rows, grad_rows], axis=-1)


def body(tokens, cotangent, expert_ids, gate_probs, w_gate, w_up, w_down):
    tok_count, features = tokens.shape
    top_count = expert_ids.shape[1]
    expert_devs = lax.axis_size("expert")
    tensor_devs = lax.axis_size("tensor")
    local_experts = w_gate.shape[0]
    all_experts = local_experts * expert_devs
    capacity = max(2, 9 * tok_count * top_count // (8 * all_experts))
    own_share = local_experts // tensor_devs
    highest = lax.Precision.HIGHEST
    matches = expert_ids[:, :, None] == jnp.arange(all_experts, dtype=jnp.int32)[None, None, :]
    chosen = jnp.sum(matches.astype(jnp.float32), axis=1)
    prob_table = jnp.sum(jnp.where(matches, gate_probs[:, :, None], 0.0), axis=1)
    positions = jnp.arange(tok_count, dtype=jnp.int32)
    earlier = (positions[:, None] > positions[None, :]).astype(jnp.float32)
    slot_table = jnp.dot(earlier, chosen, precision=highest)
    slot_ids = jnp.arange(capacity, dtype=jnp.float32)
    place = jnp.where(
        chosen.T[:, None, :] > 0.5,
        (slot_table.T[:, None, :] == slot_ids[None, :, None]).astype(jnp.float32),
        0.0,
    )
    token_rows = jnp.einsum(
        "est,td->esd", place.astype(jnp.bfloat16), tokens, preferred_element_type=jnp.float32
    ).astype(jnp.bfloat16)
    place_prob = place * prob_table.T[:, None, :]
    scaled_rows = jnp.einsum(
        "est,td->esd", place_prob, cotangent.astype(jnp.float32), precision=highest
    ).astype(jnp.bfloat16)
    buffer = jnp.concatenate([token_rows, scaled_rows], axis=-1)
    buffer = buffer.reshape(expert_devs, local_experts, capacity, 2 * features)
    arrived = lax.all_to_all(buffer, "expert", split_axis=0, concat_axis=0, tiled=True)
    results = expert_work(arrived, w_gate, w_up, w_down, features)
    reduced = lax.psum_scatter(
        results.astype(jnp.bfloat16), "tensor", scatter_dimension=1, tiled=True
    )
    returned_rows = lax.all_to_all(reduced, "expert", split_axis=0, concat_axis=0, tiled=True)
    row_total = expert_devs * own_share * capacity
    returned_rows = returned_rows.reshape(row_total, 2 * features)
    tensor_place = lax.axis_index("tensor")
    chosen_mine = lax.dynamic_slice_in_dim(
        chosen.reshape(tok_count, expert_devs, tensor_devs, own_share), tensor_place, 1, 2
    )[:, :, 0, :]
    slot_mine = lax.dynamic_slice_in_dim(
        slot_table.reshape(tok_count, expert_devs, tensor_devs, own_share), tensor_place, 1, 2
    )[:, :, 0, :]
    prob_mine = lax.dynamic_slice_in_dim(
        prob_table.reshape(tok_count, expert_devs, tensor_devs, own_share), tensor_place, 1, 2
    )[:, :, 0, :]
    collect = jnp.where(
        chosen_mine[..., None] > 0.5,
        (slot_mine[..., None] == slot_ids[None, None, None, :]).astype(jnp.float32),
        0.0,
    )
    collect_prob = (collect * prob_mine[..., None]).reshape(tok_count, row_total)
    collect = collect.reshape(tok_count, row_total)
    output_part = jnp.dot(
        collect_prob, returned_rows[:, :features].astype(jnp.float32), precision=highest
    )
    input_part = jnp.dot(
        collect.astype(jnp.bfloat16),
        returned_rows[:, features:],
        preferred_element_type=jnp.float32,
    )
    mixed, grad_tokens = (
        lax.psum(output_part.astype(jnp.bfloat16), "tensor").astype(jnp.float32),
        lax.psum(input_part.astype(jnp.bfloat16), "tensor").astype(jnp.float32),
    )
    return (mixed.astype(jnp.bfloat16), grad_tokens.astype(jnp.bfloat16))


def solution(mesh):
    return jax.shard_map(
        body,
        mesh=mesh,
        in_specs=(
            P("expert", None),
            P("expert", None),
            P("expert", None),
            P("expert", None),
            P("expert", "tensor", None),
            P("expert", "tensor", None),
            P("expert", "tensor", None),
        ),
        out_specs=(P("expert", None), P("expert", None)),
        check_vma=False,
    )
```

profile of v0, /device:TPU:1, one launch (start us, length us, event | category | flops | bytes accessed | tf_op | source)
XLA Modules:
  0.0 604.0 jit_solution(26834078855225393)
XLA Ops:
  7.2 0.0 copy-start
  7.2 0.0 copy-start.2
  7.2 0.0 reduce-scatter.2.cloned.1.call-start
  7.2 0.9 copy.37
  8.2 0.8 copy.40
  8.9 0.4 convert_reduce_fusion
  9.3 0.2 fusion.49
  9.6 0.1 copy.42
  9.7 0.1 copy.43
  9.8 0.0 copy-done
  9.8 2.8 convolution_convert_fusion.1
  12.6 0.0 copy-done.2
  12.6 9.5 %convolution_convert_fusion = bf16[128,9,4096]{2,0,1:T(8,128)(2,1)} fusion(bf16[128,4096]{1,0:T(8,128)(2,1)S(1)} %copy-done.2, f32[128,128]{1,0:T(8,128)S(1)} %copy.43, f32[128,128]{1,0:T(8,128)S(1)} %bitcast.69, pred[128,128]{1,0:T(8,128)(4,1)S(1)} %copy.42), kind=kOutput, calls=%fused_computation.11 | convolution fusion | flops 7253065728 | bytes 10633216 | tf_op jit(solution)/shard_map/est,td->esd/dot_general | solution.py:56
  22.2 7.2 %maximum_bitcast_fusion = bf16[16,8,9,8192]{3,1,0,2:T(8,128)(2,1)S(1)} fusion(bf16[128,9,4096]{2,0,1:T(8,128)(2,1)} %convolution_convert_fusion, bf16[128,9,4096]{2,0,1:T(8,128)(2,1)S(1)} %convolution_convert_fusion.1), kind=kLoop, calls=%fused_computation | loop fusion | flops 37748736 | bytes 37748736 | tf_op jit(solution)/shard_map/reshape | solution.py:60
  29.4 6.6 %copy.44 = bf16[16,8,9,8192]{3,1,2,0:T(8,128)(2,1)} copy(bf16[16,8,9,8192]{3,1,0,2:T(8,128)(2,1)S(1)} %maximum_bitcast_fusion) | data formatting | bytes 37748736 | tf_op jit(solution)/shard_map/reshape | solution.py:60
  36.0 215.5 %all_to_all.10 = bf16[16,8,9,8192]{3,1,2,0:T(8,128)(2,1)S(1)} all-to-all(bf16[16,8,9,8192]{3,1,2,0:T(8,128)(2,1)} %copy.44), channel_id=1, replica_groups=mesh['expert'=16,'tensor'=8] {'expert'}, dimensions={0} | all-to-all | bytes 37748736 | tf_op jit(solution)/shard_map/all_to_all | solution.py:61
  251.6 7.1 %fusion.60 = (bf16[16,8,9,4096]{3,1,2,0:T(8,128)(2,1)}, bf16[16,8,9,4096]{3,1,2,0:T(8,128)(2,1)}) fusion(bf16[16,8,9,8192]{3,1,2,0:T(8,128)(2,1)S(1)} %all_to_all.10), kind=kLoop, calls=%fused_computation.69 | loop fusion | bytes 37748736 | tf_op jit(solution)/shard_map/slice | solution.py:9
  258.7 11.8 %fusion.14 = f32[16,8,9,112]{3,0,2,1:T(8,128)S(1)} fusion(bf16[8,112,4096]{2,1,0:T(8,128)(2,1)} %param.11, bf16[16,8,9,4096]{3,1,2,0:T(8,128)(2,1)} %get-tuple-element.7), kind=kOutput, calls=%fused_computation.22 | convolution fusion | flops 1056964608 | bytes 17293312 | tf_op jit(solution)/shard_map/sicd,ihd->sich/dot_general | solution.py:10
  270.5 11.9 %fusion.19 = f32[16,8,9,112]{3,0,2,1:T(8,128)S(1)} fusion(bf16[8,112,4096]{2,1,0:T(8,128)(2,1)} %param.12, bf16[16,8,9,4096]{3,1,2,0:T(8,128)(2,1)} %get-tuple-element.7), kind=kOutput, calls=%fused_computation.23 | convolution fusion | flops 1056964608 | bytes 17293312 | tf_op jit(solution)/shard_map/sicd,ihd->sich/dot_general | solution.py:11
  282.3 11.7 %fusion.24 = f32[16,8,9,112]{3,0,2,1:T(8,128)S(1)} fusion(bf16[8,112,4096]{2,1,0:T(8,128)(2,1)} %param.13, bf16[16,8,9,4096]{3,1,2,0:T(8,128)(2,1)} %get-tuple-element.6), kind=kOutput, calls=%fused_computation.24 | convolution fusion | flops 1056964608 | bytes 17293312 | tf_op jit(solution)/shard_map/sicd,ihd->sich/dot_general | solution.py:16
  294.0 9.4 %convert_bitcast_fusion = bf16[16,8,9,4096]{3,0,2,1:T(8,128)(2,1)} fusion(bf16[8,112,4096]{2,1,0:T(8,128)(2,1)} %param.13, f32[16,8,9,112]{3,0,2,1:T(8,128)S(1)} %fusion.19, f32[16,8,9,112]{3,0,2,1:T(8,128)S(1)} %fusion.14), kind=kOutput, calls=%fused_computation.6 | convolution fusion | flops 1062457344 | bytes 17809408 | tf_op jit(solution)/shard_map/sich,ihd->sicd/dot_general | solution.py:15
  303.5 12.2 %fusion.9 = f32[8,16,9,4096]{3,1,2,0:T(8,128)} fusion(bf16[8,112,4096]{2,1,0:T(8,128)(2,1)} %param.11, f32[16,8,9,112]{3,0,2,1:T(8,128)S(1)} %fusion.14, f32[16,8,9,112]{3,0,2,1:T(8,128)S(1)} %fusion.24, f32[16,8,9,112]{3,0,2,1:T(8,128)S(1)} %fusion.19), kind=kOutput, calls=%fused_computation.15 | convolution fusion | flops 1058254848 | bytes 27762688 | tf_op jit(solution)/shard_map/sich,ihd->sicd/dot_general | solution.py:23
  315.6 15.0 %fusion = bf16[16,8,9,4096]{3,0,2,1:T(8,128)(2,1)} fusion(f32[8,16,9,4096]{3,1,2,0:T(8,128)} %fusion.9, bf16[8,112,4096]{2,1,0:T(8,128)(2,1)} %param.12, f32[16,8,9,112]{3,0,2,1:T(8,128)S(1)} %fusion.24, f32[16,8,9,112]{3,0,2,1:T(8,128)S(1)} %fusion.14), kind=kOutput, calls=%fused_computation.3 | convolution fusion | flops 1067175936 | bytes 36683776 | tf_op jit(solution)/shard_map/sich,ihd->sicd/dot_general | solution.py:24
  330.6 16.5 %pad_maximum_fusion = bf16[16,8,9,8192]{3,0,2,1:T(8,128)(2,1)} fusion(bf16[16,8,9,4096]{3,0,2,1:T(8,128)(2,1)} %fusion, bf16[16,8,9,4096]{3,0,2,1:T(8,128)(2,1)} %convert_bitcast_fusion), kind=kLoop, calls=%fused_computation.1 | loop fusion | flops 37748736 | bytes 37748736 | tf_op jit(solution)/shard_map/concatenate | solution.py:27
  347.1 0.0 reduce-scatter.2.cloned.1.call-update
  347.1 100.2 %reduce-scatter.2.cloned.1.call-done = bf16[16,1,9,8192]{3,0,2,1:T(8,128)(2,1)} async-done(((bf16[16,8,9,8192]{3,0,2,1:T(8,128)(2,1)}), bf16[16,1,9,8192]{3,0,2,1:T(8,128)(2,1)}) %reduce-scatter.2.cloned.1.call-update) | async-done | bytes 2359312 | tf_op jit(solution)/shard_map/reduce_scatter | solution.py:63
  447.3 5.2 copy.47
  452.5 6.7 %all-to-all-start.1 = ((bf16[16,1,9,8192]{3,2,1,0:T(8,128)(2,1)}), bf16[16,1,9,8192]{3,2,1,0:T(8,128)(2,1)}, u32[]{:S(2)}, u32[]{:S(2)}) async-start(bf16[16,1,9,8192]{3,2,1,0:T(8,128)(2,1)} %copy.47), calls=%async_computation.2 | async-start | bytes 8388608 | tf_op jit(solution)/shard_map/all_to_all | solution.py:66
  459.2 0.0 copy-start.1
  459.2 0.0 all-reduce.3.cloned.1.call-start
  459.2 0.1 copy.41
  459.3 0.1 copy.38
  459.5 0.1 eq.59
  459.7 0.1 broadcast_compare_fusion
  459.8 59.8 %all-to-all-done.1 = bf16[16,1,9,8192]{3,2,1,0:T(8,128)(2,1)} async-done(((bf16[16,1,9,8192]{3,2,1,0:T(8,128)(2,1)}), bf16[16,1,9,8192]{3,2,1,0:T(8,128)(2,1)}, u32[]{:S(2)}, u32[]{:S(2)}) %all-to-all-start.1) | async-done | bytes 2359328 | tf_op jit(solution)/shard_map/all_to_all | solution.py:66
  519.7 2.8 reshape.49
  522.5 1.5 convolution_convert_fusion.2
  523.9 2.0 convolution_convert_fusion.3
  525.9 0.0 all-reduce.3.cloned.1.call-update
  526.0 66.4 %all-reduce.3.cloned.1.call-done = (bf16[128,4096]{1,0:T(8,128)(2,1)}, bf16[128,4096]{1,0:T(8,128)(2,1)}) async-done(((bf16[128,4096]{1,0:T(8,128)(2,1)}, bf16[128,4096]{1,0:T(8,128)(2,1)}), (bf16[128,4096]{1,0:T(8,128)(2,1)}, bf16[128,4096]{1,0:T(8,128)(2,1)})) %all-reduce.3.cloned.1.call-update) | async-done | bytes 2097168 | tf_op jit(solution)/shard_map/psum | solution.py:95
  592.4 2.3 copy.71
  594.7 2.3 copy.72
  596.9 0.0 copy-done.1
  (11 shorter events, 0.2 us)
Async XLA Ops:
  7.2 2.7 copy-start
  7.2 5.4 copy-start.2
  7.2 440.1 %reduce-scatter.2.cloned.1.call-start = ((), (), s32[]{:S(2)}) async-start(), calls=%async_computation.3 | async-start | bytes 21233664 | tf_op jit(solution)/shard_map/reduce_scatter | solution.py:63
  452.5 67.2 %all-to-all-start.1 = ((bf16[16,1,9,8192]{3,2,1,0:T(8,128)(2,1)}), bf16[16,1,9,8192]{3,2,1,0:T(8,128)(2,1)}, u32[]{:S(2)}, u32[]{:S(2)}) async-start(bf16[16,1,9,8192]{3,2,1,0:T(8,128)(2,1)} %copy.47), calls=%async_computation.2 | async-start | bytes 8388608 | tf_op jit(solution)/shard_map/all_to_all | solution.py:66
  459.2 137.8 %copy-start.1 = (bf16[128,4096]{1,0:T(8,128)(2,1)S(1)}, bf16[128,4096]{1,0:T(8,128)(2,1)}, u32[]{:S(2)}) copy-start(bf16[128,4096]{1,0:T(8,128)(2,1)} %param.7) | copy-start | bytes 3145732
  459.2 133.2 %all-reduce.3.cloned.1.call-start = ((), (), s32[]{:S(2)}) async-start(), calls=%async_computation.4 | async-start | bytes 4194304 | tf_op jit(solution)/shard_map/psum | solution.py:95
Sparse Core Ops, SparseCore 0:
  347.2 100.0 reduce-scatter.1
  526.1 66.2 all-reduce.2
where the time goes:
time: 610 us; the launch traced here: 604 us
  waiting for transfers between devices  226 us (37%)
  blocking collectives  216 us (35%)
  matrix products  87.9 us (14%)
  local copies, waits for them, and re-layouts  28.6 us (5%)
  other arithmetic  24.2 us (4%)
  between operations  14.5 us (2%)
  starting transfers between devices  6.79 us (1%)
    all_to_all x1, blocking collectives, body(): lax.all_to_all(buffer, 'expert', split_axis=0, concat_axis=0, tiled=True)  216 us
    reduce_scatter x1, waiting for transfers between devices, body(): lax.psum_scatter(results.astype(jnp.bfloat16), 'tensor', scatter_dimensio...  100 us
    psum x1, waiting for transfers between devices, body(): lax.psum(output_part.astype(jnp.bfloat16), 'tensor').astype(jnp.float32)  66.4 us
    all_to_all x1, waiting for transfers between devices, body(): lax.all_to_all(reduced, 'expert', split_axis=0, concat_axis=0, tiled=True)  59.8 us
    concatenate x1, other arithmetic, expert_work(): return jnp.concatenate([output_rows, grad_rows], axis=-1)  16.5 us
    dot_general x1, matrix products, expert_work(): jnp.einsum('sich,ihd->sicd', grad_up, w_up, preferred_element_type=jnp.fl...  15 us
  transfers between devices with their start and end apart: 3, of which 3 were waited for; matrix products, arithmetic and copies ran while one was open for 0% of the time, Pallas kernels for 0%

commit v1 on v0

v1 whole, which is shorter than its diff:
```python
import jax
import jax.numpy as jnp
from jax import lax
from jax.experimental import pallas as pl
from jax.experimental.pallas import tpu as pltpu
from jax.sharding import PartitionSpec as P

BF = jnp.bfloat16
F32 = jnp.float32
RING = 4
PEERS = 16
SLOTS = 8
MESH = pl.DeviceIdType.MESH


def flat_rows(block):
    groups, rows, width = block.shape
    return block.astype(F32).reshape(groups * rows, width).astype(BF)


def kernel(
    send, coll_hi, coll_lo, coll_one, perm, perm_back, wg, wu, wd,
    mixed_ref, grad_ref,
    x, wv, xs, xov, acc, accx, hid, rel, own_in, ret, comb, fin,
    a2a_s, a2a_r, ag_s, ag_r, rl_s, rl_r, wl, wx_s, wx_r,
    ac_s, ac_r, hd_s, hd_r, h_s, h_r, o_s, o_r, b_s, b_r, fy_s, fy_r, fs_s, fs_r,
):
    e, t = lax.axis_index("expert"), lax.axis_index("tensor")
    ez, ex = e // RING, e % RING
    y, c = t // 2, t % 2
    right_y, left_y, far_y = (y + 1) % RING, (y + 3) % RING, (y + 2) % RING
    right, left, sib = right_y * 2 + c, left_y * 2 + c, y * 2 + 1 - c
    half = xs.shape[1] // 2
    core_width = half * RING

    def to_of(k):
        return ((ez + k // RING) % RING) * RING + (ex + k % RING) % RING

    def from_of(k):
        return ((ez + RING - k // RING) % RING) * RING + (ex + RING - k % RING) % RING

    def remote(src, dst, ssem, rsem, pe, pt):
        return pltpu.make_async_remote_copy(
            src_ref=src, dst_ref=dst, send_sem=ssem, recv_sem=rsem,
            device_id={"expert": pe, "tensor": pt}, device_id_type=MESH,
        )

    mats = (wg, wu, wd)
    hu = wg.shape[1]

    def w_local(g, v):
        cols = pl.ds(pl.multiple_of(c * core_width + v * half, half), half)
        return pltpu.make_async_copy(
            mats[g].at[:, :, cols], wv.at[g, v, :, pl.ds(0, hu), :], wl.at[g, v]
        )

    def w_cross(g, v):
        cols = pl.ds(pl.multiple_of((1 - c) * core_width + v * half, half), half)
        return remote(
            mats[g].at[:, :, cols], wv.at[g, v, :, pl.ds(128, hu), :],
            wx_s.at[g, v], wx_r.at[g, v], e, sib,
        )

    for g in range(3):
        for v in range(RING):
            w_local(g, v).start()

    barrier = pltpu.get_barrier_semaphore()

    @pl.loop(1, PEERS)
    def _(k):
        pl.semaphore_signal(
            barrier, inc=1, device_id={"expert": to_of(k), "tensor": t}, device_id_type=MESH
        )

    for other in (right, left, sib):
        pl.semaphore_signal(
            barrier, inc=1, device_id={"expert": e, "tensor": other}, device_id_type=MESH
        )
    pl.semaphore_wait(barrier, PEERS + 2)

    def a2a(k):
        dst = to_of(k)
        return remote(send.at[dst], x.at[y, :, e], a2a_s.at[k], a2a_r.at[k], dst, t)

    def a2a_in(k):
        return remote(send.at[e], x.at[y, :, from_of(k)], a2a_s.at[k], a2a_r.at[k], to_of(k), t)

    first = pltpu.make_async_copy(send.at[e], x.at[y, :, e], a2a_r.at[0])
    first.start()

    @pl.loop(1, PEERS)
    def _(k):
        a2a(k).start()

    for v in range(RING):
        for g in range(3):
            w_cross(g, v).start()

    zeros = jnp.zeros((8, 16, half), BF)
    for g in range(3):
        for v in range(RING):
            wv[g, v, :, hu:128, :] = zeros
            wv[g, v, :, 128 + hu:256, :] = zeros

    def go_right(k):
        s = from_of(k)
        return remote(x.at[y, :, s], x.at[y, :, s], ag_s.at[0, k], ag_r.at[0, k], e, right)

    def go_left(k):
        s = from_of(k)
        return remote(x.at[y, :, s], x.at[y, :, s], ag_s.at[1, k], ag_r.at[1, k], e, left)

    def from_left(k):
        s = from_of(k)
        return remote(x.at[y, :, s], x.at[left_y, :, s], ag_s.at[0, k], ag_r.at[0, k], e, right)

    def from_right(k):
        s = from_of(k)
        return remote(x.at[y, :, s], x.at[right_y, :, s], ag_s.at[1, k], ag_r.at[1, k], e, left)

    def relay_right(k):
        s = from_of(k)
        return remote(x.at[left_y, :, s], x.at[left_y, :, s], rl_s.at[k], rl_r.at[k], e, right)

    def relay_left(k):
        s = from_of(k)
        return remote(x.at[right_y, :, s], x.at[right_y, :, s], rl_s.at[k], rl_r.at[k], e, left)

    def relay_in(k):
        s = from_of(k)
        return remote(x.at[left_y, :, s], x.at[far_y, :, s], rl_s.at[k], rl_r.at[k], e, right)

    first.wait()
    go_right(0).start()
    go_left(0).start()

    @pl.loop(1, PEERS)
    def _(k):
        a2a_in(k).wait_recv()
        go_right(k).start()
        go_left(k).start()

    for v in range(RING):
        for g in range(3):
            w_local(g, v).wait()
            w_cross(g, v).wait_recv()

    def acc_swap(i):
        return remote(
            acc.at[:, i, :, pl.ds(128, 128)], accx.at[:, i], ac_s.at[i], ac_r.at[i], e, sib
        )

    def contract(v, start, end):
        xov[...] = jnp.dot(perm[...], flat_rows(x[v, 8]), preferred_element_type=F32).astype(BF)

        @pl.loop(0, 8)
        def _(i):
            xs[0:128, :] = flat_rows(x[v, i])
            xs[128:144, :] = xov[pl.ds(pl.multiple_of(i * 16, 16), 16), :]
            for g in range(3):
                rows = xs[:, 0:half] if g < 2 else xs[:, half:]
                part = lax.dot_general(
                    rows, wv[g, v, i], (((1,), (1,)), ((), ())), preferred_element_type=F32
                )
                if start:
                    acc[g, i] = part
                else:
                    acc[g, i] = acc[g, i] + part
            if end:
                acc_swap(i).start()

    contract(y, True, False)

    @pl.loop(0, PEERS // 2)
    def _(j):
        even, odd = 2 * j, 2 * j + 1
        from_left(even).wait_recv()
        relay_right(even).start()
        from_right(even).wait_recv()
        from_right(odd).wait_recv()
        relay_left(odd).start()
        from_left(odd).wait_recv()

    contract(left_y, False, False)
    contract(right_y, False, False)

    @pl.loop(0, PEERS)
    def _(k):
        relay_in(k).wait_recv()

    contract(far_y, False, True)

    @pl.loop(0, PEERS)
    def _(k):
        go_right(k).wait_send()
        go_left(k).wait_send()
        relay_right(k).wait_send()

    def hid_swap(i):
        return remote(
            hid.at[:, i, :, pl.ds(0, 128)], hid.at[:, i, :, pl.ds(128, 128)],
            hd_s.at[i], hd_r.at[i], e, sib,
        )

    @pl.loop(0, 8)
    def _(i):
        acc_swap(i).wait_recv()
        pre = acc[0, i, :, 0:128] + accx[0, i]
        up = acc[1, i, :, 0:128] + accx[1, i]
        gh = acc[2, i, :, 0:128] + accx[2, i]
        sg = jax.nn.sigmoid(pre)
        act = pre * sg
        hid[0, i, :, 0:128] = (act * up).astype(BF)
        hid[1, i, :, 0:128] = (gh * up * sg * (1.0 + pre * (1.0 - sg))).astype(BF)
        hid[2, i, :, 0:128] = (gh * act).astype(BF)
        hid_swap(i).start()

    @pl.loop(0, 8)
    def _(i):
        hid_swap(i).wait_recv()

    def expand(v):
        @pl.loop(0, 8)
        def _(i):
            out = jnp.dot(hid[0, i], wv[2, v, i], preferred_element_type=F32)
            x[v, i, :, :, 0:half] = out[0:128].reshape(PEERS, SLOTS, half).astype(BF)
            tail = pl.ds(pl.multiple_of(i * 16, 16), 16)
            xov[tail, 0:half] = out[128:144].astype(BF)
            grad = jnp.dot(hid[1, i], wv[0, v, i], preferred_element_type=F32)
            grad = grad + jnp.dot(hid[2, i], wv[1, v, i], preferred_element_type=F32)
            x[v, i, :, :, half:] = grad[0:128].reshape(PEERS, SLOTS, half).astype(BF)
            xov[tail, half:] = grad[128:144].astype(BF)

        over = jnp.dot(perm_back[...], xov[...], preferred_element_type=F32)
        x[v, 8] = over.reshape(PEERS, SLOTS, 2 * half).astype(BF)

    def far_right(k):
        return remote(x.at[far_y, :, from_of(k)], rel.at[k], h_s.at[k], h_r.at[k], e, right)

    def far_left(k):
        return remote(x.at[far_y, :, from_of(k)], rel.at[k], h_s.at[k], h_r.at[k], e, left)

    def near_right(k):
        return remote(
            x.at[right_y, :, from_of(k)], own_in.at[0, k], o_s.at[0, k], o_r.at[0, k], e, right
        )

    def near_left(k):
        return remote(
            x.at[left_y, :, from_of(k)], own_in.at[1, k], o_s.at[1, k], o_r.at[1, k], e, left
        )

    expand(far_y)

    @pl.loop(0, PEERS // 2)
    def _(j):
        far_right(2 * j).start()
        far_left(2 * j + 1).start()

    expand(right_y)

    @pl.loop(0, PEERS // 2)
    def _(j):
        near_right(2 * j + 1).start()

    expand(left_y)

    @pl.loop(0, PEERS // 2)
    def _(j):
        near_left(2 * j).start()

    expand(y)

    @pl.loop(0, PEERS // 2)
    def _(j):
        even, odd = 2 * j, 2 * j + 1
        far_right(even).wait_recv()
        s = from_of(even)
        x[right_y, :, s] = (x[right_y, :, s].astype(F32) + rel[even].astype(F32)).astype(BF)
        near_right(even).start()
        far_left(odd).wait_recv()
        s = from_of(odd)
        x[left_y, :, s] = (x[left_y, :, s].astype(F32) + rel[odd].astype(F32)).astype(BF)
        near_left(odd).start()

    def back(k):
        s = from_of(k)
        return remote(x.at[y, :, s], ret.at[e], b_s.at[k], b_r.at[k], s, t)

    def back_in(k):
        return remote(x.at[y, :, e], ret.at[to_of(k)], b_s.at[k], b_r.at[k], from_of(k), t)

    def own_sum(k):
        near_right(k).wait_recv()
        near_left(k).wait_recv()
        total = x[y, :, from_of(k)].astype(F32) + own_in[0, k].astype(F32)
        return (total + own_in[1, k].astype(F32)).astype(BF)

    ret[e] = own_sum(0)

    @pl.loop(1, PEERS)
    def _(k):
        x[y, :, from_of(k)] = own_sum(k)
        back(k).start()

    def combine(d):
        rows = flat_rows(ret[d])
        low = rows[:, 0:half]
        part = jnp.dot(coll_hi[d], low, preferred_element_type=F32)
        part = part + jnp.dot(coll_lo[d], low, preferred_element_type=F32)
        return part, jnp.dot(coll_one[d], rows[:, half:], preferred_element_type=F32)

    comb[:, 0:half], comb[:, half:] = combine(e)

    @pl.loop(1, PEERS)
    def _(k):
        back_in(k).wait_recv()
        m, g = combine(to_of(k))
        comb[:, 0:half] = comb[:, 0:half] + m
        comb[:, half:] = comb[:, half:] + g

    fin[t] = comb[...].astype(BF)

    rows_a, rows_b = pl.ds(0, 64), pl.ds(64, 64)
    left_t, right_t, far_t = left, right, far_y * 2 + c

    def fin_y(n, slot, rows, peer):
        ref = fin.at[slot, rows, :]
        return remote(ref, ref, fy_s.at[n], fy_r.at[n], e, peer)

    def fin_s(n, slot, rows):
        ref = fin.at[slot, rows, :]
        return remote(ref, ref, fs_s.at[n], fs_r.at[n], e, sib)

    full = pl.ds(0, 128)
    out_right, out_left = fin_y(0, t, full, right), fin_y(1, t, full, left)
    out_right.start()
    out_left.start()
    sends = [fin_s(0, t, full)]
    sends[0].start()
    fin_y(0, left_t, full, right).wait_recv()
    hop_right = fin_y(2, left_t, rows_a, right)
    hop_right.start()
    sends.append(fin_s(1, left_t, full))
    sends[1].start()
    fin_y(1, right_t, full, left).wait_recv()
    hop_left = fin_y(3, right_t, rows_b, left)
    hop_left.start()
    sends.append(fin_s(2, right_t, full))
    sends[2].start()
    fin_y(2, far_t, rows_a, right).wait_recv()
    sends.append(fin_s(3, far_t, rows_a))
    sends[3].start()
    fin_y(3, far_t, rows_b, left).wait_recv()
    sends.append(fin_s(4, far_t, rows_b))
    sends[4].start()
    for copy in sends:
        copy.wait()
    for copy in (out_right, out_left, hop_right, hop_left):
        copy.wait_send()

    @pl.loop(1, PEERS)
    def _(k):
        a2a(k).wait_send()
        back(k).wait_send()

    @pl.loop(0, PEERS)
    def _(k):
        far_right(k).wait_send()
        near_right(k).wait_send()
        near_left(k).wait_send()

    @pl.loop(0, 8)
    def _(i):
        acc_swap(i).wait_send()
        hid_swap(i).wait_send()

    for g in range(3):
        for v in range(RING):
            w_cross(g, v).wait_send()

    for slot in range(2 * RING):
        off = (slot % 2) * core_width + (slot // 2) * half
        mixed_ref[:, off:off + half] = fin[slot, :, 0:half]
        grad_ref[:, off:off + half] = fin[slot, :, half:]


def expert_kernel(send, coll_hi, coll_lo, coll_one, perm, perm_back, w_gate, w_up, w_down):
    width = send.shape[-1]
    half = width // 2
    tok = coll_hi.shape[1]
    features = w_gate.shape[2]
    dma = pltpu.SemaphoreType.DMA
    vmem = pl.BlockSpec(memory_space=pltpu.VMEM)
    hbm = pl.BlockSpec(memory_space=pltpu.HBM)
    return pl.pallas_call(
        kernel,
        out_shape=[jax.ShapeDtypeStruct((tok, features), BF)] * 2,
        in_specs=[vmem] * 6 + [hbm] * 3,
        out_specs=[vmem] * 2,
        scratch_shapes=[
            pltpu.VMEM((RING, 9, PEERS, SLOTS, width), BF),
            pltpu.VMEM((3, RING, 8, 256, half), BF),
            pltpu.VMEM((144, width), BF),
            pltpu.VMEM((128, width), BF),
            pltpu.VMEM((3, 8, 144, 256), F32),
            pltpu.VMEM((3, 8, 144, 128), F32),
            pltpu.VMEM((3, 8, 144, 256), BF),
            pltpu.VMEM((PEERS, 9, SLOTS, width), BF),
            pltpu.VMEM((2, PEERS, 9, SLOTS, width), BF),
            pltpu.VMEM((PEERS, 9, SLOTS, width), BF),
            pltpu.VMEM((tok, width), F32),
            pltpu.VMEM((2 * RING, tok, width), BF),
            dma((PEERS,)), dma((PEERS,)),
            dma((2, PEERS)), dma((2, PEERS)),
            dma((PEERS,)), dma((PEERS,)),
            dma((3, RING)), dma((3, RING)), dma((3, RING)),
            dma((8,)), dma((8,)), dma((8,)), dma((8,)),
            dma((PEERS,)), dma((PEERS,)),
            dma((2, PEERS)), dma((2, PEERS)),
            dma((PEERS,)), dma((PEERS,)),
            dma((4,)), dma((4,)), dma((5,)), dma((5,)),
        ],
        compiler_params=pltpu.CompilerParams(
            collective_id=0, has_side_effects=True, vmem_limit_bytes=66 * 1000 * 1000
        ),
    )(send, coll_hi, coll_lo, coll_one, perm, perm_back, w_gate, w_up, w_down)


def by_group(table, devs):
    experts, cap, tok = table.shape
    table = table.reshape(devs, experts // devs, cap, tok)
    main = table[:, :, :8].reshape(devs, (experts // devs) * 8, tok)
    return jnp.concatenate([main, table[:, :, 8]], axis=1)


def body(tokens, cotangent, expert_ids, gate_probs, w_gate, w_up, w_down):
    tok_count, features = tokens.shape
    devs = lax.axis_size("expert")
    local_experts = w_gate.shape[0]
    all_experts = local_experts * devs
    cap = 9
    slices = 2 * RING
    half = features // slices
    t = lax.axis_index("tensor")
    offset = (t % 2) * (features // 2) + (t // 2) * half
    matches = expert_ids[:, :, None] == jnp.arange(all_experts, dtype=jnp.int32)[None, None, :]
    chosen = jnp.any(matches, axis=1)
    prob_table = jnp.sum(jnp.where(matches, gate_probs[:, :, None], 0.0), axis=1)
    positions = jnp.arange(tok_count, dtype=jnp.int32)
    earlier = (positions[:, None] > positions[None, :]).astype(BF)
    slot_table = jnp.dot(earlier, chosen.astype(BF), preferred_element_type=F32)
    slot_ids = jnp.arange(cap, dtype=F32)
    place = chosen.T[:, None, :] & (slot_table.T[:, None, :] == slot_ids[None, :, None])
    place = by_group(place, devs)
    prob_rows = by_group(
        jnp.broadcast_to(prob_table.T[:, None, :], (all_experts, cap, tok_count)), devs
    )
    weights = jnp.where(place, prob_rows, 0.0)
    row_prob = jnp.sum(weights, axis=-1, keepdims=True)
    one = place.astype(BF)
    tok_part = lax.dynamic_slice_in_dim(tokens, offset, half, 1)
    cot_part = lax.dynamic_slice_in_dim(cotangent, offset, half, 1)
    token_rows = jnp.einsum("dst,tf->dsf", one, tok_part, preferred_element_type=F32).astype(BF)
    cot_rows = jnp.einsum("dst,tf->dsf", one, cot_part, preferred_element_type=F32)
    scaled_rows = (cot_rows * row_prob).astype(BF)
    send = jnp.concatenate([token_rows, scaled_rows], axis=-1)
    send = send.reshape(devs, cap, SLOTS, 2 * half)
    weights = weights.transpose(0, 2, 1)
    rounded = lax.reduce_precision(weights, 8, 7)
    coll_hi = rounded.astype(BF)
    coll_lo = (weights - rounded).astype(BF)
    coll_one = one.transpose(0, 2, 1)
    order = jnp.arange(devs * local_experts, dtype=jnp.int32)
    source = (order % devs) * local_experts + order // devs
    perm = (source[:, None] == order[None, :]).astype(BF)
    return tuple(
        expert_kernel(send, coll_hi, coll_lo, coll_one, perm, perm.T, w_gate, w_up, w_down)
    )


def solution(mesh):
    return jax.shard_map(
        body,
        mesh=mesh,
        in_specs=(
            P("expert", None),
            P("expert", None),
            P("expert", None),
            P("expert", None),
            P("expert", "tensor", None),
            P("expert", "tensor", None),
            P("expert", "tensor", None),
        ),
        out_specs=(P("expert", None), P("expert", None)),
        check_vma=False,
    )
```

time: 610 us -> 240 us (0.39)
  waiting for transfers between devices: 226 us -> 0 us
  blocking collectives: 216 us -> 0 us
  Pallas kernels: 0 us -> 214 us
  matrix products: 87.9 us -> 3.21 us
  local copies, waits for them, and re-layouts: 28.6 us -> 12.8 us
  other arithmetic: 24.2 us -> 8.92 us
  between operations: 14.5 us -> 0.76 us
  starting transfers between devices: 6.79 us -> 0 us
    all_to_all x1 -> x0, blocking collectives: 216 us -> none  [body(): lax.all_to_all(buffer, 'expert', split_axis=0, concat_axis=0, tiled=True)]
    pallas_call x0 -> x1, Pallas kernels: none -> 214 us  [expert_kernel(): pl.pallas_call(kernel, out_shape=[jax.ShapeDtypeStruct((tok, features), B...]
    reduce_scatter x1 -> x0, waiting for transfers between devices: 100 us -> none  [body(): lax.psum_scatter(results.astype(jnp.bfloat16), 'tensor', scatter_dimensio...]
    dot_general x11 -> x3, matrix products: 87.9 us -> 3.21 us  [the longest x1 1.45 us: body(): jnp.einsum('dst,tf->dsf', one, cot_part, preferred_element_type=F32)]
    psum x1 -> x0, waiting for transfers between devices: 66.4 us -> none  [body(): lax.psum(output_part.astype(jnp.bfloat16), 'tensor').astype(jnp.float32)]
    all_to_all x1 -> x0, waiting for transfers between devices: 59.8 us -> none  [body(): lax.all_to_all(reduced, 'expert', split_axis=0, concat_axis=0, tiled=True)]
    concatenate x1 -> x0, other arithmetic: 16.5 us -> none  [expert_work(): return jnp.concatenate([output_rows, grad_rows], axis=-1)]
    reshape x2 -> x3, local copies, waits for them, and re-layouts: 9.42 us -> 0.74 us  [by_group(): main = table[:, :, :8].reshape(devs, experts // devs * 8, tok)]
  transfers between devices with their start and end apart: 3 -> 0, of which waited for: 3 -> 0; matrix products, arithmetic and copies ran while one was open for 0% -> 0% of each run, Pallas kernels for 0% -> 0%
where the time goes in v1:
time: 240 us
  Pallas kernels  214 us (89%)
  local copies, waits for them, and re-layouts  12.8 us (5%)
  other arithmetic  8.92 us (4%)
  matrix products  3.21 us (1%)
    pallas_call x1, Pallas kernels, expert_kernel(): pl.pallas_call(kernel, out_shape=[jax.ShapeDtypeStruct((tok, features), B...  214 us
    slice x2, local copies, waits for them, and re-layouts, by_group(): main = table[:, :, :8].reshape(devs, experts // devs * 8, tok)  6.19 us

profile of v1, /device:TPU:1, one launch (start us, length us, event | category | flops | bytes accessed | tf_op | source)
XLA Modules:
  0.0 239.6 jit_solution(10955887095846336120)
XLA Ops:
  0.7 0.8 copy.37
  1.4 0.3 fusion.2
  1.7 0.1 copy.38
  1.8 0.3 fusion.8
  2.2 1.1 copy.39
  3.2 2.5 %fusion = pred[16,8,9,128]{1,3,0,2:T(32,128)(4,1)S(1)} fusion(f32[16,8,128]{1,2,0:T(8,128)S(1)} %fusion.8, pred[16,8,128]{1,2,0:T(8,128)(4,1)} %copy.39), kind=kLoop, calls=%fused_computation.1 | loop fusion | flops 294912 | bytes 229376 | tf_op jit(solution)/shard_map/and | solution.py:455
  5.7 2.3 slice.13
  8.0 0.0 copy-start.1
  8.0 3.9 %copy.41 = pred[16,8,8,128]{3,2,1,0:T(8,128)(4,1)S(1)} copy(pred[16,8,8,128]{1,3,0,2:T(8,128)(4,1)} %slice.13) | data formatting | bytes 262144 | tf_op jit(solution)/shard_map/slice | solution.py:434
  11.9 0.4 copy.42
  12.3 1.2 convert_bitcast_fusion
  13.5 0.0 copy-done.1
  13.5 0.1 copy.45
  13.6 0.3 select_reduce_fusion
  13.9 0.1 copy.46
  14.0 0.1 broadcast_bitcast_fusion
  14.1 0.3 copy.47
  14.4 0.3 copy.48
  14.8 1.2 fusion.1
  16.0 0.1 reduce_sum.19
  16.1 1.5 multiply_convert_fusion
  17.5 1.4 convolution_convert_fusion
  19.0 1.8 maximum_bitcast_fusion.send
  20.7 0.9 reduce-precision_convert_fusion.coll_hi
  21.6 0.7 fusion.11
  22.3 213.9 %shard_map.86 = (bf16[128,4096]{1,0:T(8,128)(2,1)}, bf16[128,4096]{1,0:T(8,128)(2,1)}) custom-call(bf16[16,9,8,1024]{3,2,1,0:T(8,128)(2,1)} %maximum_bitcast_fusion.send, bf16[16,128,72]{2,1,0:T(8,128)(2,1)} %reduce-precision_convert_fusion.coll_hi, bf16[16,128,72]{2,1,0:T(8,128)(2,1)} %get-tuple-element.4.coll_lo, ...), custom_call_target="tpu_custom_call" | custom-call | tf_op jit(solution)/shard_map/pallas_call | solution.py:397
  236.2 0.0 copy-start
  236.2 2.4 copy.62
  238.6 0.0 copy-done
  238.6 1.0 copy.63
  (2 shorter events, 0.0 us)
Async XLA Ops:
  8.0 5.5 %copy-start.1 = (f32[128,8]{0,1:T(8,128)S(1)}, f32[128,8]{0,1:T(8,128)}, u32[]{:S(2)}) copy-start(f32[128,8]{0,1:T(8,128)} %param.10) | copy-start | bytes 12292
  236.2 2.4 copy-start

commit v2 on v1

v2 whole, which is shorter than its diff:
```python
import jax
import jax.numpy as jnp
from jax import lax
from jax.experimental import pallas as pl
from jax.experimental.pallas import tpu as pltpu
from jax.sharding import PartitionSpec as P

BF = jnp.bfloat16
F32 = jnp.float32
RING = 4
PEERS = 16
SLOTS = 8
AXIAL = 6
DIAG = 9
ROWS = 72
MESH = pl.DeviceIdType.MESH


def flat_rows(block):
    return block.astype(F32).reshape(-1, block.shape[-1]).astype(BF)


def kernel(
    tokens, cotangent, ids_ref, probs_ref, perm, perm_back, wg, wu, wd,
    mixed_ref, grad_ref,
    tok, cot, slot_ref, prob_ref, one_d, wrow_d, wrow_g, coll_d, coll_g,
    sendg, sendd, x, wv, xs, xov, acc, accx, hid, rel, own_in, ret, retd, comb, combs, combr, fin,
    tk, g_s, g_r, d_s, d_r, ag_s, ag_r, rl_s, rl_r, wl, wx_s, wx_r,
    ac_s, ac_r, hd_s, hd_r, h_s, h_r, o_s, o_r, b_s, b_r, rd_s, rd_r, cs_s, cs_r,
    fy_s, fy_r, fs_s, fs_r, out_sem,
):
    e, t = lax.axis_index("expert"), lax.axis_index("tensor")
    ez, ex = e // RING, e % RING
    y, c = t // 2, t % 2
    right_y, left_y, far_y = (y + 1) % RING, (y + 3) % RING, (y + 2) % RING
    right, left, sib, far = right_y * 2 + c, left_y * 2 + c, y * 2 + 1 - c, far_y * 2 + c
    half = xs.shape[1] // 2
    core_width = half * RING

    def to_of(k):
        return ((ez + k // RING) % RING) * RING + (ex + k % RING) % RING

    def from_of(k):
        return ((ez + RING - k // RING) % RING) * RING + (ex + RING - k % RING) % RING

    def axial(j):
        return (j % 3 + 1) * (1 + 3 * (j // 3))

    def diag(j):
        return (1 + j // 3) * RING + 1 + j % 3

    def remote(src, dst, ssem, rsem, pe, pt):
        return pltpu.make_async_remote_copy(
            src_ref=src, dst_ref=dst, send_sem=ssem, recv_sem=rsem,
            device_id={"expert": pe, "tensor": pt}, device_id_type=MESH,
        )

    def signal(pe, pt):
        pl.semaphore_signal(
            pltpu.get_barrier_semaphore(), inc=1,
            device_id={"expert": pe, "tensor": pt}, device_id_type=MESH,
        )

    mats = (wg, wu, wd)
    hu = wg.shape[1]

    def columns(core, v):
        return pl.ds(pl.multiple_of(core * core_width + v * half, half), half)

    def w_local(g, v):
        return pltpu.make_async_copy(
            mats[g].at[:, :, columns(c, v)], wv.at[g, v, :, pl.ds(0, hu), :], wl.at[g, v]
        )

    def w_cross(g, v):
        return remote(
            mats[g].at[:, :, columns(1 - c, v)], wv.at[g, v, :, pl.ds(128, hu), :],
            wx_s.at[g, v], wx_r.at[g, v], e, sib,
        )

    def t_local(n, v):
        src, dst = ((tokens, tok), (cotangent, cot))[n]
        return pltpu.make_async_copy(src.at[:, columns(c, v)], dst.at[v], tk.at[n, v])

    for v in range(RING):
        for n in range(2):
            t_local(n, v).start()

    @pl.loop(1, PEERS)
    def _(k):
        signal(to_of(k), t)

    for other in (right, left, far, sib):
        signal(e, other)

    for g in range(3):
        for v in range(RING):
            w_local(g, v).start()

    count = ids_ref.shape[0]
    lane = lax.broadcasted_iota(jnp.int32, (count, count), 1)
    line = lax.broadcasted_iota(jnp.int32, (count, count), 0)
    chosen = jnp.zeros((count, count), F32)
    prob = jnp.zeros((count, count), F32)
    for k in range(ids_ref.shape[1]):
        match = ids_ref[:, k:k + 1] == lane
        chosen = chosen + match.astype(F32)
        prob = prob + jnp.where(match, probs_ref[:, k:k + 1], 0.0)
    chosen = chosen.T
    before = (line < lane).astype(F32).astype(BF)
    slot = jnp.dot(chosen.astype(BF), before, preferred_element_type=F32)
    slot_ref[...] = jnp.where(chosen > 0.5, slot, -1.0)
    prob_ref[...] = prob.T

    def row_block(j):
        return pl.ds(pl.multiple_of(j * ROWS, SLOTS), ROWS)

    def build(d):
        block = pl.ds(pl.multiple_of(d * SLOTS, SLOTS), SLOTS)
        slots, weights = slot_ref[block, :], prob_ref[block, :]
        number = lax.broadcasted_iota(jnp.int32, (SLOTS, count), 0).astype(F32)
        place, weight = [], []
        for i in range(SLOTS):
            hit = slots[i:i + 1, :] == number
            place.append(hit.astype(F32))
            weight.append(jnp.where(hit, weights[i:i + 1, :], 0.0))
        hit = slots == float(SLOTS)
        place.append(hit.astype(F32))
        weight.append(jnp.where(hit, weights, 0.0))
        return jnp.concatenate(place, axis=0), jnp.concatenate(weight, axis=0)

    def fill(ref, one, weight, v):
        total = jnp.sum(weight, axis=1, keepdims=True)
        rows = jnp.dot(one, tok[v], preferred_element_type=F32)
        ref[:, :, 0:half] = rows.reshape(9, SLOTS, half).astype(BF)
        rows = jnp.dot(one, cot[v], preferred_element_type=F32) * total
        ref[:, :, half:] = rows.reshape(9, SLOTS, half).astype(BF)

    for n in range(2):
        for v in range(RING):
            t_local(n, v).wait()

    @pl.loop(0, DIAG)
    def _(j):
        place, weight = build(to_of(diag(j)))
        wrow_g[j // 3, row_block(j % 3), :] = weight
        fill(sendg.at[j], place.astype(BF), weight, y)

    pl.semaphore_wait(pltpu.get_barrier_semaphore(), PEERS + 3)

    def slice_out(j):
        return remote(sendg.at[j], x.at[y, :, e], g_s.at[j], g_r.at[j], to_of(diag(j)), t)

    def slice_in(j):
        s = from_of(diag(j))
        return remote(sendg.at[j], x.at[y, :, s], g_s.at[j], g_r.at[j], to_of(diag(j)), t)

    def whole_out(j, v):
        return remote(
            sendd.at[v, j], x.at[v, :, e], d_s.at[v, j], d_r.at[v, j], to_of(axial(j)), t
        )

    def whole_in(j, v):
        s = from_of(axial(j))
        return remote(
            sendd.at[v, j], x.at[v, :, s], d_s.at[v, j], d_r.at[v, j], to_of(axial(j)), t
        )

    @pl.loop(0, DIAG)
    def _(j):
        slice_out(j).start()

    @pl.loop(0, AXIAL)
    def _(j):
        place, weight = build(to_of(axial(j)))
        wrow_d[row_block(j), :] = weight
        one_d[j] = place.astype(BF)
        fill(sendd.at[y, j], one_d[j], weight, y)
        whole_out(j, y).start()

    for v in range(RING):
        for g in range(3):
            w_cross(g, v).start()

    def pushed(n, j, dst_y, peer):
        s = from_of(diag(j))
        return remote(x.at[y, :, s], x.at[dst_y, :, s], ag_s.at[n, j], ag_r.at[n, j], e, peer)

    def go_right(j):
        return pushed(0, j, y, right)

    def go_left(j):
        return pushed(1, j, y, left)

    def from_left(j):
        return pushed(0, j, left_y, right)

    def from_right(j):
        return pushed(1, j, right_y, left)

    def relay(j, slice_y, peer):
        s = from_of(diag(j))
        ref = x.at[slice_y, :, s]
        return remote(ref, ref, rl_s.at[j], rl_r.at[j], e, peer)

    @pl.loop(0, DIAG)
    def _(j):
        slice_in(j).wait_recv()
        go_right(j).start()
        go_left(j).start()
        for u in range(2):
            n = 2 * j + u
            q, jj = 1 + n // AXIAL, n % AXIAL
            v = (y + 2 * q - 1 - 3 * (q // 3)) % RING
            fill(sendd.at[v, jj], one_d[jj], wrow_d[row_block(jj), :], v)
            whole_out(jj, v).start()

    place, weight = build(e)
    wrow_d[row_block(AXIAL), :] = weight
    place = place.astype(BF)
    for v in range(RING):
        fill(x.at[v, :, e], place, weight, v)

    zeros = jnp.zeros((8, 16, half), BF)
    for g in range(3):
        for v in range(RING):
            wv[g, v, :, hu:128, :] = zeros
            wv[g, v, :, 128 + hu:256, :] = zeros

    for v in range(RING):
        for g in range(3):
            w_local(g, v).wait()
            w_cross(g, v).wait_recv()

    def acc_swap(i):
        return remote(
            acc.at[:, i, :, pl.ds(128, 128)], accx.at[:, i], ac_s.at[i], ac_r.at[i], e, sib
        )

    def contract(v, start, end):
        @pl.loop(0, AXIAL)
        def _(j):
            whole_in(j, v).wait_recv()

        xov[...] = jnp.dot(perm[...], flat_rows(x[v, 8]), preferred_element_type=F32).astype(BF)

        @pl.loop(0, 8)
        def _(i):
            xs[0:128, :] = flat_rows(x[v, i])
            xs[128:144, :] = xov[pl.ds(pl.multiple_of(i * 16, 16), 16), :]
            for g in range(3):
                rows = xs[:, 0:half] if g < 2 else xs[:, half:]
                part = lax.dot_general(
                    rows, wv[g, v, i], (((1,), (1,)), ((), ())), preferred_element_type=F32
                )
                if start:
                    acc[g, i] = part
                else:
                    acc[g, i] = acc[g, i] + part
            if end:
                acc_swap(i).start()

    def relay_even(j):
        from_left(j).wait_recv()
        relay(j, left_y, right).start()
        from_right(j).wait_recv()

    def relay_odd(j):
        from_right(j).wait_recv()
        relay(j, right_y, left).start()
        from_left(j).wait_recv()

    contract(y, True, False)

    @pl.loop(0, DIAG // 2)
    def _(j):
        relay_even(2 * j)
        relay_odd(2 * j + 1)

    relay_even(DIAG - 1)
    contract(right_y, False, False)
    contract(left_y, False, False)

    @pl.loop(0, DIAG)
    def _(j):
        relay(j, far_y, right).wait_recv()

    contract(far_y, False, True)

    @pl.loop(0, DIAG)
    def _(j):
        go_right(j).wait_send()
        go_left(j).wait_send()
        relay(j, left_y, right).wait_send()

    def hid_swap(i):
        return remote(
            hid.at[:, i, :, pl.ds(0, 128)], hid.at[:, i, :, pl.ds(128, 128)],
            hd_s.at[i], hd_r.at[i], e, sib,
        )

    @pl.loop(0, 8)
    def _(i):
        acc_swap(i).wait()
        pre = acc[0, i, :, 0:128] + accx[0, i]
        up = acc[1, i, :, 0:128] + accx[1, i]
        gh = acc[2, i, :, 0:128] + accx[2, i]
        sg = jax.nn.sigmoid(pre)
        act = pre * sg
        hid[0, i, :, 0:128] = (act * up).astype(BF)
        hid[1, i, :, 0:128] = (gh * up * sg * (1.0 + pre * (1.0 - sg))).astype(BF)
        hid[2, i, :, 0:128] = (gh * act).astype(BF)
        hid_swap(i).start()

    @pl.loop(0, 8)
    def _(i):
        hid_swap(i).wait_recv()

    def whole_back(j, v):
        s = from_of(axial(j))
        return remote(x.at[v, :, s], retd.at[v, j], rd_s.at[v, j], rd_r.at[v, j], s, t)

    def expand(v):
        @pl.loop(0, 8)
        def _(i):
            out = jnp.dot(hid[0, i], wv[2, v, i], preferred_element_type=F32)
            x[v, i, :, :, 0:half] = out[0:128].reshape(PEERS, SLOTS, half).astype(BF)
            tail = pl.ds(pl.multiple_of(i * 16, 16), 16)
            xov[tail, 0:half] = out[128:144].astype(BF)
            grad = jnp.dot(hid[1, i], wv[0, v, i], preferred_element_type=F32)
            grad = grad + jnp.dot(hid[2, i], wv[1, v, i], preferred_element_type=F32)
            x[v, i, :, :, half:] = grad[0:128].reshape(PEERS, SLOTS, half).astype(BF)
            xov[tail, half:] = grad[128:144].astype(BF)

        over = jnp.dot(perm_back[...], xov[...], preferred_element_type=F32)
        x[v, 8] = over.reshape(PEERS, SLOTS, 2 * half).astype(BF)

    def return_whole(v):
        @pl.loop(0, AXIAL)
        def _(j):
            whole_back(j, v).start()

    def far_out(j, peer):
        s = from_of(diag(j))
        return remote(x.at[far_y, :, s], rel.at[j], h_s.at[j], h_r.at[j], e, peer)

    def near(n, j, slice_y, peer):
        s = from_of(diag(j))
        return remote(x.at[slice_y, :, s], own_in.at[n, j], o_s.at[n, j], o_r.at[n, j], e, peer)

    def near_right(j):
        return near(0, j, right_y, right)

    def near_left(j):
        return near(1, j, left_y, left)

    def add_relayed(j, slice_y):
        far_out(j, right).wait_recv()
        s = from_of(diag(j))
        x[slice_y, :, s] = (x[slice_y, :, s].astype(F32) + rel[j].astype(F32)).astype(BF)

    expand(far_y)

    @pl.loop(0, DIAG // 2)
    def _(j):
        far_out(2 * j, right).start()
        far_out(2 * j + 1, left).start()

    far_out(DIAG - 1, right).start()
    return_whole(far_y)
    expand(right_y)
    near_right(1).start()
    return_whole(right_y)
    expand(left_y)
    near_left(0).start()
    return_whole(left_y)
    expand(y)
    return_whole(y)

    @pl.loop(0, DIAG // 2)
    def _(j):
        even, odd = 2 * j, 2 * j + 1
        add_relayed(even, right_y)
        near_right(even).start()
        near_left(even + 2).start()
        add_relayed(odd, left_y)
        near_left(odd).start()

        @pl.when(j < DIAG // 2 - 1)
        def _():
            near_right(odd + 2).start()

    add_relayed(DIAG - 1, right_y)
    near_right(DIAG - 1).start()

    def split(ref, weights):
        weights = weights.T
        hi = weights.astype(BF)
        ref[0] = hi
        ref[1] = (weights - hi.astype(F32)).astype(BF)
        ref[2] = (weights > 0.0).astype(F32).astype(BF)

    def gathered(coll, rows):
        width = rows.shape[0]
        low = rows[:, 0:half]
        part = jnp.dot(coll[0, :, 0:width], low, preferred_element_type=F32)
        part = part + jnp.dot(coll[1, :, 0:width], low, preferred_element_type=F32)
        return part, jnp.dot(coll[2, :, 0:width], rows[:, half:], preferred_element_type=F32)

    wrow_d[(AXIAL + 1) * ROWS:, :] = jnp.zeros((wrow_d.shape[0] - (AXIAL + 1) * ROWS, count), F32)
    split(coll_d, wrow_d[...])
    for n in range(3):
        wrow_g[n, 3 * ROWS:, :] = jnp.zeros((wrow_g.shape[1] - 3 * ROWS, count), F32)
        split(coll_g.at[n], wrow_g[n])

    def part_sum(n, slice_y):
        return remote(combs.at[n], combr.at[n], cs_s.at[n], cs_r.at[n], e, slice_y * 2 + c)

    for n, v in enumerate((far_y, right_y, left_y, y)):
        retd[v, AXIAL] = x[v, :, e]

        @pl.loop(0, AXIAL)
        def _(j, v=v):
            whole_back(j, v).wait_recv()

        m, g = gathered(coll_d, flat_rows(retd[v]))
        if n < 3:
            combs[n, :, 0:half] = m.astype(BF)
            combs[n, :, half:] = g.astype(BF)
            part_sum(n, v).start()
        else:
            comb[:, 0:half] = m
            comb[:, half:] = g

    def slice_back(j):
        s = from_of(diag(j))
        return remote(x.at[y, :, s], ret.at[j], b_s.at[j], b_r.at[j], s, t)

    @pl.loop(0, DIAG)
    def _(j):
        near_right(j).wait_recv()
        near_left(j).wait_recv()
        s = from_of(diag(j))
        total = x[y, :, s].astype(F32) + own_in[0, j].astype(F32)
        x[y, :, s] = (total + own_in[1, j].astype(F32)).astype(BF)
        slice_back(j).start()

    for n, v in enumerate((far_y, right_y, left_y)):
        part_sum(n, v).wait_recv()
        comb[...] = comb[...] + combr[n].astype(F32)
    for n in range(3):
        for j in range(3 * n, 3 * n + 3):
            slice_back(j).wait_recv()
        m, g = gathered(coll_g.at[n], flat_rows(ret[3 * n:3 * n + 3]))
        comb[:, 0:half] = comb[:, 0:half] + m
        comb[:, half:] = comb[:, half:] + g
    fin[t] = comb[...].astype(BF)

    rows_of = (pl.ds(0, 64), pl.ds(64, 64))

    def fin_copy(sems, n, slot_t, h, peer):
        ref = fin.at[slot_t, rows_of[h], :]
        return remote(ref, ref, sems[0].at[n], sems[1].at[n], e, peer)

    yy, ss = (fy_s, fy_r), (fs_s, fs_r)
    sends = []

    def push(sems, n, slot_t, h, peer):
        copy = fin_copy(sems, n, slot_t, h, peer)
        copy.start()
        sends.append(copy)

    push(yy, 0, t, 0, right)
    push(yy, 1, t, 1, left)
    push(yy, 2, t, 1, right)
    push(yy, 3, t, 0, left)
    push(ss, 0, t, 0, sib)
    push(ss, 1, t, 1, sib)
    fin_copy(yy, 0, left, 0, right).wait_recv()
    push(yy, 4, left, 0, right)
    push(ss, 2, left, 0, sib)
    fin_copy(yy, 1, right, 1, left).wait_recv()
    push(yy, 5, right, 1, left)
    push(ss, 3, right, 1, sib)
    fin_copy(yy, 2, left, 1, right).wait_recv()
    push(ss, 4, left, 1, sib)
    fin_copy(yy, 3, right, 0, left).wait_recv()
    push(ss, 5, right, 0, sib)
    fin_copy(yy, 4, far, 0, right).wait_recv()
    push(ss, 6, far, 0, sib)
    fin_copy(yy, 5, far, 1, left).wait_recv()
    push(ss, 7, far, 1, sib)

    outs = []

    def put(slot_t, owner_c, owner_y):
        for n, ref in enumerate((mixed_ref, grad_ref)):
            copy = pltpu.make_async_copy(
                fin.at[slot_t, :, pl.ds(n * half, half)], ref.at[:, columns(owner_c, owner_y)],
                out_sem.at[len(outs)],
            )
            copy.start()
            outs.append(copy)

    for owner_y in (y, left_y, right_y, far_y):
        put(owner_y * 2 + c, c, owner_y)
    for n, (owner_y, h) in enumerate(
        ((y, 0), (y, 1), (left_y, 0), (right_y, 1), (left_y, 1), (right_y, 0), (far_y, 0), (far_y, 1))
    ):
        fin_copy(ss, n, owner_y * 2 + 1 - c, h, sib).wait_recv()
    for owner_y in (y, left_y, right_y, far_y):
        put(owner_y * 2 + 1 - c, 1 - c, owner_y)

    for copy in sends:
        copy.wait_send()

    @pl.loop(0, DIAG)
    def _(j):
        slice_out(j).wait_send()
        far_out(j, right).wait_send()
        near_right(j).wait_send()
        near_left(j).wait_send()
        slice_back(j).wait_send()

    @pl.loop(0, AXIAL)
    def _(j):
        for v in range(RING):
            whole_out(j, v).wait_send()
            whole_back(j, v).wait_send()

    @pl.loop(0, 8)
    def _(i):
        hid_swap(i).wait_send()

    for g in range(3):
        for v in range(RING):
            w_cross(g, v).wait_send()
    for n, v in enumerate((far_y, right_y, left_y)):
        part_sum(n, v).wait_send()
    for copy in outs:
        copy.wait()


def expert_kernel(tokens, cotangent, ids, probs, perm, perm_back, w_gate, w_up, w_down):
    tok, features = tokens.shape
    half = features // (2 * RING)
    width = 2 * half
    dma = pltpu.SemaphoreType.DMA
    vmem = pl.BlockSpec(memory_space=pltpu.VMEM)
    hbm = pl.BlockSpec(memory_space=pltpu.HBM)
    return pl.pallas_call(
        kernel,
        out_shape=[jax.ShapeDtypeStruct((tok, features), BF)] * 2,
        in_specs=[hbm] * 2 + [vmem] * 4 + [hbm] * 3,
        out_specs=[hbm] * 2,
        scratch_shapes=[
            pltpu.VMEM((RING, tok, half), BF),
            pltpu.VMEM((RING, tok, half), BF),
            pltpu.VMEM((tok, tok), F32),
            pltpu.VMEM((tok, tok), F32),
            pltpu.VMEM((AXIAL, ROWS, tok), BF),
            pltpu.VMEM((512, tok), F32),
            pltpu.VMEM((3, 256, tok), F32),
            pltpu.VMEM((3, tok, 512), BF),
            pltpu.VMEM((3, 3, tok, 256), BF),
            pltpu.VMEM((DIAG, 9, SLOTS, width), BF),
            pltpu.VMEM((RING, AXIAL, 9, SLOTS, width), BF),
            pltpu.VMEM((RING, 9, PEERS, SLOTS, width), BF),
            pltpu.VMEM((3, RING, 8, 256, half), BF),
            pltpu.VMEM((144, width), BF),
            pltpu.VMEM((128, width), BF),
            pltpu.VMEM((3, 8, 144, 256), F32),
            pltpu.VMEM((3, 8, 144, 128), F32),
            pltpu.VMEM((3, 8, 144, 256), BF),
            pltpu.VMEM((DIAG, 9, SLOTS, width), BF),
            pltpu.VMEM((2, DIAG, 9, SLOTS, width), BF),
            pltpu.VMEM((DIAG, 9, SLOTS, width), BF),
            pltpu.VMEM((RING, AXIAL + 1, 9, SLOTS, width), BF),
            pltpu.VMEM((tok, width), F32),
            pltpu.VMEM((3, tok, width), BF),
            pltpu.VMEM((3, tok, width), BF),
            pltpu.VMEM((2 * RING, tok, width), BF),
            dma((2, RING)),
            dma((DIAG,)), dma((DIAG,)),
            dma((RING, AXIAL)), dma((RING, AXIAL)),
            dma((2, DIAG)), dma((2, DIAG)),
            dma((DIAG,)), dma((DIAG,)),
            dma((3, RING)), dma((3, RING)), dma((3, RING)),
            dma((8,)), dma((8,)), dma((8,)), dma((8,)),
            dma((DIAG,)), dma((DIAG,)),
            dma((2, DIAG)), dma((2, DIAG)),
            dma((DIAG,)), dma((DIAG,)),
            dma((RING, AXIAL)), dma((RING, AXIAL)),
            dma((3,)), dma((3,)),
            dma((6,)), dma((6,)), dma((8,)), dma((8,)),
            dma((4 * RING,)),
        ],
        compiler_params=pltpu.CompilerParams(
            collective_id=0, has_side_effects=True, vmem_limit_bytes=67_000_000
        ),
    )(tokens, cotangent, ids, probs, perm, perm_back, w_gate, w_up, w_down)


def body(tokens, cotangent, expert_ids, gate_probs, w_gate, w_up, w_down):
    devs = lax.axis_size("expert")
    local_experts = w_gate.shape[0]
    order = jnp.arange(devs * local_experts, dtype=jnp.int32)
    source = (order % devs) * local_experts + order // devs
    perm = (source[:, None] == order[None, :]).astype(BF)
    return tuple(
        expert_kernel(
            tokens, cotangent, expert_ids, gate_probs, perm, perm.T, w_gate, w_up, w_down
        )
    )


def solution(mesh):
    return jax.shard_map(
        body,
        mesh=mesh,
        in_specs=(
            P("expert", None),
            P("expert", None),
            P("expert", None),
            P("expert", None),
            P("expert", "tensor", None),
            P("expert", "tensor", None),
            P("expert", "tensor", None),
        ),
        out_specs=(P("expert", None), P("expert", None)),
        check_vma=False,
    )
```

time: 240 us -> 162 us (0.68)
  Pallas kernels: 214 us -> 152 us
  other arithmetic: 8.92 us -> 0.69 us
  local copies, waits for them, and re-layouts: 12.8 us -> 7.4 us
  matrix products: 3.21 us -> 0 us
    pallas_call x1, Pallas kernels: 214 us -> 152 us  [expert_kernel(): pl.pallas_call(kernel, out_shape=[jax.ShapeDtypeStruct((tok, features), B...]
    slice x2 -> x0, local copies, waits for them, and re-layouts: 6.19 us -> none  [by_group(): main = table[:, :, :8].reshape(devs, experts // devs * 8, tok)]
    dot_general x3 -> x0, matrix products: 3.21 us -> none  [the longest x1 1.45 us: body(): jnp.einsum('dst,tf->dsf', one, cot_part, preferred_element_type=F32)]
    unnamed x8 -> x4, local copies, waits for them, and re-layouts: 4.24 us -> 7.4 us
    and x1 -> x0, other arithmetic: 2.51 us -> none  [body(): chosen.T[:, None, :] & (slot_table.T[:, None, :] == slot_ids[None, :, None])]
where the time goes in v2:
time: 162 us; the launch traced here: 161 us
  Pallas kernels  152 us (94%)
  local copies, waits for them, and re-layouts  7.4 us (5%)
    pallas_call x1, Pallas kernels, expert_kernel(): pl.pallas_call(kernel, out_shape=[jax.ShapeDtypeStruct((tok, features), B...  152 us
    unnamed x4, local copies, waits for them, and re-layouts  7.4 us

profile of v2, /device:TPU:1, one launch (start us, length us, event | category | flops | bytes accessed | tf_op | source)
XLA Modules:
  0.0 161.1 jit_solution(4100988929106224228)
XLA Ops:
  0.6 0.7 fusion.1
  1.3 1.4 copy.9.ids_ref
  2.7 1.4 copy.10.probs_ref
  4.2 152.3 %shard_map.86 = (bf16[128,4096]{1,0:T(8,128)(2,1)}, bf16[128,4096]{1,0:T(8,128)(2,1)}) custom-call(bf16[128,4096]{1,0:T(8,128)(2,1)} %tokens.1, bf16[128,4096]{1,0:T(8,128)(2,1)} %cotangent.1, s32[128,8]{1,0:T(8,128)} %copy.9.ids_ref, f32[128,8]{1,0:T(8,128)} %copy.10.probs_ref, bf16[128,128]{1,0:T(8,128)(2,1)} %get-tuple-element.3.perm, ...), custom_call_target="tpu_custom_call" | custom-call | tf_op jit(solution)/shard_map/pallas_call | solution.py:551
  156.5 2.3 %copy.13 = bf16[128,4096]{1,0:T(8,128)(2,1)} copy(bf16[128,4096]{1,0:T(8,128)(2,1)} %get-tuple-element.6) | data formatting | bytes 2097152
  158.8 2.3 %copy.14 = bf16[128,4096]{1,0:T(8,128)(2,1)} copy(bf16[128,4096]{1,0:T(8,128)(2,1)} %get-tuple-element.7) | data formatting | bytes 2097152
  (1 shorter events, 0.0 us)

commit v3 on v2

--- a/solution.py
+++ b/solution.py
@@ -21,12 +21,12 @@
 
 
 def kernel(
-    tokens, cotangent, ids_ref, probs_ref, perm, perm_back, wg, wu, wd,
+    tokens, cotangent, ids_ref, probs_ref, wg, wu, wd,
     mixed_ref, grad_ref,
-    tok, cot, slot_ref, prob_ref, one_d, wrow_d, wrow_g, coll_d, coll_g,
-    sendg, sendd, x, wv, xs, xov, acc, accx, hid, rel, own_in, ret, retd, comb, combs, combr, fin,
+    tok, cot, perm, perm_back, slot_ref, prob_ref, one_d, wrow_d, wrow_g, coll_d, coll_g,
+    sendg, sendd, x, wv, xs, xov, acc, accx, hid, rel, own_in, ret, retd, comb, combs, combr, combf, combh, fin,
     tk, g_s, g_r, d_s, d_r, ag_s, ag_r, rl_s, rl_r, wl, wx_s, wx_r,
-    ac_s, ac_r, hd_s, hd_r, h_s, h_r, o_s, o_r, b_s, b_r, rd_s, rd_r, cs_s, cs_r,
+    ac_s, ac_r, hd_s, hd_r, h_s, h_r, o_s, o_r, b_s, b_r, rd_s, rd_r, cs_s, cs_r, ch_s, ch_r,
     fy_s, fy_r, fs_s, fs_r, out_sem,
 ):
     e, t = lax.axis_index("expert"), lax.axis_index("tensor")
@@ -90,27 +90,28 @@
     def _(k):
         signal(to_of(k), t)
 
-    for other in (right, left, far, sib):
+    for other in (right, left, sib):
         signal(e, other)
 
     for g in range(3):
         for v in range(RING):
             w_local(g, v).start()
 
-    count = ids_ref.shape[0]
+    count = ids_ref.shape[1]
     lane = lax.broadcasted_iota(jnp.int32, (count, count), 1)
     line = lax.broadcasted_iota(jnp.int32, (count, count), 0)
     chosen = jnp.zeros((count, count), F32)
     prob = jnp.zeros((count, count), F32)
-    for k in range(ids_ref.shape[1]):
-        match = ids_ref[:, k:k + 1] == lane
+    for k in range(ids_ref.shape[0]):
+        match = ids_ref[k:k + 1, :] == line
         chosen = chosen + match.astype(F32)
-        prob = prob + jnp.where(match, probs_ref[:, k:k + 1], 0.0)
-    chosen = chosen.T
+        prob = prob + jnp.where(match, probs_ref[k:k + 1, :], 0.0)
     before = (line < lane).astype(F32).astype(BF)
     slot = jnp.dot(chosen.astype(BF), before, preferred_element_type=F32)
     slot_ref[...] = jnp.where(chosen > 0.5, slot, -1.0)
-    prob_ref[...] = prob.T
+    prob_ref[...] = prob
+    perm[...] = (lane == (line & 15) * SLOTS + (line >> 4)).astype(F32).astype(BF)
+    perm_back[...] = (line == (lane & 15) * SLOTS + (lane >> 4)).astype(F32).astype(BF)
 
     def row_block(j):
         return pl.ds(pl.multiple_of(j * ROWS, SLOTS), ROWS)
@@ -146,7 +147,13 @@
         wrow_g[j // 3, row_block(j % 3), :] = weight
         fill(sendg.at[j], place.astype(BF), weight, y)
 
-    pl.semaphore_wait(pltpu.get_barrier_semaphore(), PEERS + 3)
+    @pl.loop(0, AXIAL)
+    def _(j):
+        place, weight = build(to_of(axial(j)))
+        wrow_d[row_block(j), :] = weight
+        one_d[j] = place.astype(BF)
+
+    pl.semaphore_wait(pltpu.get_barrier_semaphore(), PEERS + 2)
 
     def slice_out(j):
         return remote(sendg.at[j], x.at[y, :, e], g_s.at[j], g_r.at[j], to_of(diag(j)), t)
@@ -170,14 +177,6 @@
     def _(j):
         slice_out(j).start()
 
-    @pl.loop(0, AXIAL)
-    def _(j):
-        place, weight = build(to_of(axial(j)))
-        wrow_d[row_block(j), :] = weight
-        one_d[j] = place.astype(BF)
-        fill(sendd.at[y, j], one_d[j], weight, y)
-        whole_out(j, y).start()
-
     for v in range(RING):
         for g in range(3):
             w_cross(g, v).start()
@@ -208,12 +207,32 @@
         slice_in(j).wait_recv()
         go_right(j).start()
         go_left(j).start()
-        for u in range(2):
-            n = 2 * j + u
-            q, jj = 1 + n // AXIAL, n % AXIAL
-            v = (y + 2 * q - 1 - 3 * (q // 3)) % RING
-            fill(sendd.at[v, jj], one_d[jj], wrow_d[row_block(jj), :], v)
-            whole_out(jj, v).start()
+
+        @pl.when(j < DIAG - 1)
+        def _():
+            for u in range(3):
+                n = 3 * j + u
+                q, jj = n // AXIAL, n % AXIAL
+                v = (y + RING + 2 * q - 1 - 3 * (q // 3) + (3 - q) // 3) % RING
+                fill(sendd.at[v, jj], one_d[jj], wrow_d[row_block(jj), :], v)
+                whole_out(jj, v).start()
+
+    def relay_even(j):
+        from_left(j).wait_recv()
+        relay(j, left_y, right).start()
+        from_right(j).wait_recv()
+
+    def relay_odd(j):
+        from_right(j).wait_recv()
+        relay(j, right_y, left).start()
+        from_left(j).wait_recv()
+
+    @pl.loop(0, DIAG // 2)
+    def _(j):
+        relay_even(2 * j)
+        relay_odd(2 * j + 1)
+
+    relay_even(DIAG - 1)
 
     place, weight = build(e)
     wrow_d[row_block(AXIAL), :] = weight
@@ -236,6 +255,24 @@
         return remote(
             acc.at[:, i, :, pl.ds(128, 128)], accx.at[:, i], ac_s.at[i], ac_r.at[i], e, sib
         )
+
+    def hid_swap(i):
+        return remote(
+            hid.at[:, i, :, pl.ds(0, 128)], hid.at[:, i, :, pl.ds(128, 128)],
+            hd_s.at[i], hd_r.at[i], e, sib,
+        )
+
+    def activate(i):
+        acc_swap(i).wait()
+        pre = acc[0, i, :, 0:128] + accx[0, i]
+        up = acc[1, i, :, 0:128] + accx[1, i]
+        gh = acc[2, i, :, 0:128] + accx[2, i]
+        sg = jax.nn.sigmoid(pre)
+        act = pre * sg
+        hid[0, i, :, 0:128] = (act * up).astype(BF)
+        hid[1, i, :, 0:128] = (gh * up * sg * (1.0 + pre * (1.0 - sg))).astype(BF)
+        hid[2, i, :, 0:128] = (gh * act).astype(BF)
+        hid_swap(i).start()
 
     def contract(v, start, end):
         @pl.loop(0, AXIAL)
@@ -260,24 +297,15 @@
             if end:
                 acc_swap(i).start()
 
-    def relay_even(j):
-        from_left(j).wait_recv()
-        relay(j, left_y, right).start()
-        from_right(j).wait_recv()
-
-    def relay_odd(j):
-        from_right(j).wait_recv()
-        relay(j, right_y, left).start()
-        from_left(j).wait_recv()
+                @pl.when(i >= 2)
+                def _():
+                    activate(i - 2)
+
+        if end:
+            activate(6)
+            activate(7)
 
     contract(y, True, False)
-
-    @pl.loop(0, DIAG // 2)
-    def _(j):
-        relay_even(2 * j)
-        relay_odd(2 * j + 1)
-
-    relay_even(DIAG - 1)
     contract(right_y, False, False)
     contract(left_y, False, False)
 
@@ -293,36 +321,15 @@
         go_left(j).wait_send()
         relay(j, left_y, right).wait_send()
 
-    def hid_swap(i):
-        return remote(
-            hid.at[:, i, :, pl.ds(0, 128)], hid.at[:, i, :, pl.ds(128, 128)],
-            hd_s.at[i], hd_r.at[i], e, sib,
-        )
-
-    @pl.loop(0, 8)
-    def _(i):
-        acc_swap(i).wait()
-        pre = acc[0, i, :, 0:128] + accx[0, i]
-        up = acc[1, i, :, 0:128] + accx[1, i]
-        gh = acc[2, i, :, 0:128] + accx[2, i]
-        sg = jax.nn.sigmoid(pre)
-        act = pre * sg
-        hid[0, i, :, 0:128] = (act * up).astype(BF)
-        hid[1, i, :, 0:128] = (gh * up * sg * (1.0 + pre * (1.0 - sg))).astype(BF)
-        hid[2, i, :, 0:128] = (gh * act).astype(BF)
-        hid_swap(i).start()
-
-    @pl.loop(0, 8)
-    def _(i):
-        hid_swap(i).wait_recv()
-
     def whole_back(j, v):
         s = from_of(axial(j))
         return remote(x.at[v, :, s], retd.at[v, j], rd_s.at[v, j], rd_r.at[v, j], s, t)
 
-    def expand(v):
+    def expand(v, start=False):
         @pl.loop(0, 8)
         def _(i):
+            if start:
+                hid_swap(i).wait_recv()
             out = jnp.dot(hid[0, i], wv[2, v, i], preferred_element_type=F32)
             x[v, i, :, :, 0:half] = out[0:128].reshape(PEERS, SLOTS, half).astype(BF)
             tail = pl.ds(pl.multiple_of(i * 16, 16), 16)
@@ -359,7 +366,7 @@
         s = from_of(diag(j))
         x[slice_y, :, s] = (x[slice_y, :, s].astype(F32) + rel[j].astype(F32)).astype(BF)
 
-    expand(far_y)
+    expand(far_y, True)
 
     @pl.loop(0, DIAG // 2)
     def _(j):
@@ -377,6 +384,47 @@
     expand(y)
     return_whole(y)
 
+    def split(ref, weights):
+        weights = weights.T
+        hi = weights.astype(BF)
+        ref[0] = hi
+        ref[1] = (weights - hi.astype(F32)).astype(BF)
+        ref[2] = (weights > 0.0).astype(F32).astype(BF)
+
+    def gathered(coll, rows):
+        width = rows.shape[0]
+        low = rows[:, 0:half]
+        part = jnp.dot(coll[0, :, 0:width], low, preferred_element_type=F32)
+        part = part + jnp.dot(coll[1, :, 0:width], low, preferred_element_type=F32)
+        return part, jnp.dot(coll[2, :, 0:width], rows[:, half:], preferred_element_type=F32)
+
+    wrow_d[(AXIAL + 1) * ROWS:, :] = jnp.zeros((wrow_d.shape[0] - (AXIAL + 1) * ROWS, count), F32)
+    split(coll_d, wrow_d[...])
+    for n in range(3):
+        wrow_g[n, 3 * ROWS:, :] = jnp.zeros((wrow_g.shape[1] - 3 * ROWS, count), F32)
+        split(coll_g.at[n], wrow_g[n])
+
+    def whole_sum(v):
+        retd[v, AXIAL] = x[v, :, e]
+
+        @pl.loop(0, AXIAL)
+        def _(j):
+            whole_back(j, v).wait_recv()
+
+        return gathered(coll_d, flat_rows(retd[v]))
+
+    def part_sum(n, peer):
+        return remote(combs.at[n], combr.at[n], cs_s.at[n], cs_r.at[n], e, peer)
+
+    def part_half(n, peer):
+        return remote(combf.at[n], combh.at[n], ch_s.at[n], ch_r.at[n], e, peer)
+
+    m, g = whole_sum(far_y)
+    combf[0] = m.astype(BF)
+    combf[1] = g.astype(BF)
+    part_half(0, right).start()
+    part_half(1, left).start()
+
     @pl.loop(0, DIAG // 2)
     def _(j):
         even, odd = 2 * j, 2 * j + 1
@@ -393,44 +441,17 @@
     add_relayed(DIAG - 1, right_y)
     near_right(DIAG - 1).start()
 
-    def split(ref, weights):
-        weights = weights.T
-        hi = weights.astype(BF)
-        ref[0] = hi
-        ref[1] = (weights - hi.astype(F32)).astype(BF)
-        ref[2] = (weights > 0.0).astype(F32).astype(BF)
-
-    def gathered(coll, rows):
-        width = rows.shape[0]
-        low = rows[:, 0:half]
-        part = jnp.dot(coll[0, :, 0:width], low, preferred_element_type=F32)
-        part = part + jnp.dot(coll[1, :, 0:width], low, preferred_element_type=F32)
-        return part, jnp.dot(coll[2, :, 0:width], rows[:, half:], preferred_element_type=F32)
-
-    wrow_d[(AXIAL + 1) * ROWS:, :] = jnp.zeros((wrow_d.shape[0] - (AXIAL + 1) * ROWS, count), F32)
-    split(coll_d, wrow_d[...])
-    for n in range(3):
-        wrow_g[n, 3 * ROWS:, :] = jnp.zeros((wrow_g.shape[1] - 3 * ROWS, count), F32)
-        split(coll_g.at[n], wrow_g[n])
-
-    def part_sum(n, slice_y):
-        return remote(combs.at[n], combr.at[n], cs_s.at[n], cs_r.at[n], e, slice_y * 2 + c)
-
-    for n, v in enumerate((far_y, right_y, left_y, y)):
-        retd[v, AXIAL] = x[v, :, e]
-
-        @pl.loop(0, AXIAL)
-        def _(j, v=v):
-            whole_back(j, v).wait_recv()
-
-        m, g = gathered(coll_d, flat_rows(retd[v]))
-        if n < 3:
-            combs[n, :, 0:half] = m.astype(BF)
-            combs[n, :, half:] = g.astype(BF)
-            part_sum(n, v).start()
-        else:
-            comb[:, 0:half] = m
-            comb[:, half:] = g
+    m, g = whole_sum(right_y)
+    part_half(0, right).wait_recv()
+    combs[0, :, 0:half] = (m + combh[0].astype(F32)).astype(BF)
+    combs[0, :, half:] = g.astype(BF)
+    part_sum(0, right).start()
+    m, g = whole_sum(left_y)
+    part_half(1, left).wait_recv()
+    combs[1, :, 0:half] = m.astype(BF)
+    combs[1, :, half:] = (g + combh[1].astype(F32)).astype(BF)
+    part_sum(1, left).start()
+    comb[:, 0:half], comb[:, half:] = whole_sum(y)
 
     def slice_back(j):
         s = from_of(diag(j))
@@ -445,8 +466,8 @@
         x[y, :, s] = (total + own_in[1, j].astype(F32)).astype(BF)
         slice_back(j).start()
 
-    for n, v in enumerate((far_y, right_y, left_y)):
-        part_sum(n, v).wait_recv()
+    for n, peer in enumerate((right, left)):
+        part_sum(n, peer).wait_recv()
         comb[...] = comb[...] + combr[n].astype(F32)
     for n in range(3):
         for j in range(3 * n, 3 * n + 3):
@@ -535,13 +556,14 @@
     for g in range(3):
         for v in range(RING):
             w_cross(g, v).wait_send()
-    for n, v in enumerate((far_y, right_y, left_y)):
-        part_sum(n, v).wait_send()
+    for n, peer in enumerate((right, left)):
+        part_sum(n, peer).wait_send()
+        part_half(n, peer).wait_send()
     for copy in outs:
         copy.wait()
 
 
-def expert_kernel(tokens, cotangent, ids, probs, perm, perm_back, w_gate, w_up, w_down):
+def expert_kernel(tokens, cotangent, ids, probs, w_gate, w_up, w_down):
     tok, features = tokens.shape
     half = features // (2 * RING)
     width = 2 * half
@@ -551,11 +573,13 @@
     return pl.pallas_call(
         kernel,
         out_shape=[jax.ShapeDtypeStruct((tok, features), BF)] * 2,
-        in_specs=[hbm] * 2 + [vmem] * 4 + [hbm] * 3,
+        in_specs=[hbm] * 2 + [vmem] * 2 + [hbm] * 3,
         out_specs=[hbm] * 2,
         scratch_shapes=[
             pltpu.VMEM((RING, tok, half), BF),
             pltpu.VMEM((RING, tok, half), BF),
+            pltpu.VMEM((tok, tok), BF),
+            pltpu.VMEM((tok, tok), BF),
             pltpu.VMEM((tok, tok), F32),
             pltpu.VMEM((tok, tok), F32),
             pltpu.VMEM((AXIAL, ROWS, tok), BF),
@@ -577,8 +601,10 @@
             pltpu.VMEM((DIAG, 9, SLOTS, width), BF),
             pltpu.VMEM((RING, AXIAL + 1, 9, SLOTS, width), BF),
             pltpu.VMEM((tok, width), F32),
-            pltpu.VMEM((3, tok, width), BF),
-            pltpu.VMEM((3, tok, width), BF),
+            pltpu.VMEM((2, tok, width), BF),
+            pltpu.VMEM((2, tok, width), BF),
+            pltpu.VMEM((2, tok, half), BF),
+            pltpu.VMEM((2, tok, half), BF),
             pltpu.VMEM((2 * RING, tok, width), BF),
             dma((2, RING)),
             dma((DIAG,)), dma((DIAG,)),
@@ -591,25 +617,20 @@
             dma((2, DIAG)), dma((2, DIAG)),
             dma((DIAG,)), dma((DIAG,)),
             dma((RING, AXIAL)), dma((RING, AXIAL)),
-            dma((3,)), dma((3,)),
+            dma((2,)), dma((2,)), dma((2,)), dma((2,)),
             dma((6,)), dma((6,)), dma((8,)), dma((8,)),
             dma((4 * RING,)),
         ],
         compiler_params=pltpu.CompilerParams(
             collective_id=0, has_side_effects=True, vmem_limit_bytes=67_000_000
         ),
-    )(tokens, cotangent, ids, probs, perm, perm_back, w_gate, w_up, w_down)
+    )(tokens, cotangent, ids, probs, w_gate, w_up, w_down)
 
 
 def body(tokens, cotangent, expert_ids, gate_probs, w_gate, w_up, w_down):
-    devs = lax.axis_size("expert")
-    local_experts = w_gate.shape[0]
-    order = jnp.arange(devs * local_experts, dtype=jnp.int32)
-    source = (order % devs) * local_experts + order // devs
-    perm = (source[:, None] == order[None, :]).astype(BF)
     return tuple(
         expert_kernel(
-            tokens, cotangent, expert_ids, gate_probs, perm, perm.T, w_gate, w_up, w_down
+            tokens, cotangent, expert_ids.T, gate_probs.T, w_gate, w_up, w_down
         )
     )
 

time: 162 us -> 166 us (1.025)
  the two profiles are of different devices: /device:TPU:1 before, /device:TPU:67 now
where the time goes in v3:
time: 166 us
  Pallas kernels  161 us (97%)
  local copies, waits for them, and re-layouts  4.57 us (3%)
    pallas_call x1, Pallas kernels, expert_kernel(): pl.pallas_call(kernel, out_shape=[jax.ShapeDtypeStruct((tok, features), B...  161 us
    unnamed x2, local copies, waits for them, and re-layouts  4.57 us

profile of v3, /device:TPU:67, one launch (start us, length us, event | category | flops | bytes accessed | tf_op | source)
XLA Modules:
  0.0 166.2 jit_solution(7801012772841568430)
XLA Ops:
  0.6 161.0 %shard_map.86 = (bf16[128,4096]{1,0:T(8,128)(2,1)}, bf16[128,4096]{1,0:T(8,128)(2,1)}) custom-call(bf16[128,4096]{1,0:T(8,128)(2,1)} %tokens.1, bf16[128,4096]{1,0:T(8,128)(2,1)} %cotangent.1, s32[8,128]{1,0:T(8,128)} %bitcast.2, f32[8,128]{1,0:T(8,128)} %bitcast.3, bf16[8,112,4096]{2,1,0:T(8,128)(2,1)} %wg.1, bf16[8,112,4096]{2,1,0:T(8,128)(2,1)} %wu.1, ...), custom_call_target="tpu_custom_call" | custom-call | tf_op jit(solution)/shard_map/pallas_call | solution.py:573
  161.6 2.3 %copy.11 = bf16[128,4096]{1,0:T(8,128)(2,1)} copy(bf16[128,4096]{1,0:T(8,128)(2,1)} %get-tuple-element.4) | data formatting | bytes 2097152
  163.9 2.3 %copy.12 = bf16[128,4096]{1,0:T(8,128)(2,1)} copy(bf16[128,4096]{1,0:T(8,128)(2,1)} %get-tuple-element.5) | data formatting | bytes 2097152

commit v4 on v3

--- a/solution.py
+++ b/solution.py
@@ -44,10 +44,11 @@
         return ((ez + RING - k // RING) % RING) * RING + (ex + RING - k % RING) % RING
 
     def axial(j):
-        return (j % 3 + 1) * (1 + 3 * (j // 3))
+        return (1 + 2 * (j // 2) - 3 * (j // 4)) * (1 + 3 * (j % 2))
 
     def diag(j):
-        return (1 + j // 3) * RING + 1 + j % 3
+        place = (4 * j) % DIAG
+        return (1 + place // 3) * RING + 1 + place % 3
 
     def remote(src, dst, ssem, rsem, pe, pt):
         return pltpu.make_async_remote_copy(
@@ -181,6 +182,9 @@
         for g in range(3):
             w_cross(g, v).start()
 
+    def turn(q):
+        return (y + RING + 2 * q - 1 - 3 * (q // 3) + (3 - q) // 3) % RING
+
     def pushed(n, j, dst_y, peer):
         s = from_of(diag(j))
         return remote(x.at[y, :, s], x.at[dst_y, :, s], ag_s.at[n, j], ag_r.at[n, j], e, peer)
@@ -212,9 +216,15 @@
         def _():
             for u in range(3):
                 n = 3 * j + u
-                q, jj = n // AXIAL, n % AXIAL
-                v = (y + RING + 2 * q - 1 - 3 * (q // 3) + (3 - q) // 3) % RING
+                v, jj = turn(n // AXIAL), n % AXIAL
                 fill(sendd.at[v, jj], one_d[jj], wrow_d[row_block(jj), :], v)
+
+        @pl.when((j >= 5) & (j < 9))
+        def _():
+            v = turn(j - 5)
+
+            @pl.loop(0, AXIAL)
+            def _(jj):
                 whole_out(jj, v).start()
 
     def relay_even(j):
@@ -451,8 +461,6 @@
     combs[1, :, 0:half] = m.astype(BF)
     combs[1, :, half:] = (g + combh[1].astype(F32)).astype(BF)
     part_sum(1, left).start()
-    comb[:, 0:half], comb[:, half:] = whole_sum(y)
-
     def slice_back(j):
         s = from_of(diag(j))
         return remote(x.at[y, :, s], ret.at[j], b_s.at[j], b_r.at[j], s, t)
@@ -466,6 +474,7 @@
         x[y, :, s] = (total + own_in[1, j].astype(F32)).astype(BF)
         slice_back(j).start()
 
+    comb[:, 0:half], comb[:, half:] = whole_sum(y)
     for n, peer in enumerate((right, left)):
         part_sum(n, peer).wait_recv()
         comb[...] = comb[...] + combr[n].astype(F32)

time: 166 us -> 150 us (0.904)
  the two profiles are of different devices: /device:TPU:67 before, /device:TPU:1 now
where the time goes in v4:
time: 150 us; the launch traced here: 149 us
  Pallas kernels  144 us (96%)
  local copies, waits for them, and re-layouts  4.57 us (3%)
    pallas_call x1, Pallas kernels, expert_kernel(): pl.pallas_call(kernel, out_shape=[jax.ShapeDtypeStruct((tok, features), B...  144 us
    unnamed x2, local copies, waits for them, and re-layouts  4.57 us

profile of v4, /device:TPU:1, one launch (start us, length us, event | category | flops | bytes accessed | tf_op | source)
XLA Modules:
  0.0 149.2 jit_solution(8750728410489860016)
XLA Ops:
  0.6 143.9 %shard_map.86 = (bf16[128,4096]{1,0:T(8,128)(2,1)}, bf16[128,4096]{1,0:T(8,128)(2,1)}) custom-call(bf16[128,4096]{1,0:T(8,128)(2,1)} %tokens.1, bf16[128,4096]{1,0:T(8,128)(2,1)} %cotangent.1, s32[8,128]{1,0:T(8,128)} %bitcast.2, f32[8,128]{1,0:T(8,128)} %bitcast.3, bf16[8,112,4096]{2,1,0:T(8,128)(2,1)} %wg.1, bf16[8,112,4096]{2,1,0:T(8,128)(2,1)} %wu.1, ...), custom_call_target="tpu_custom_call" | custom-call | tf_op jit(solution)/shard_map/pallas_call | solution.py:582
  144.6 2.3 %copy.11 = bf16[128,4096]{1,0:T(8,128)(2,1)} copy(bf16[128,4096]{1,0:T(8,128)(2,1)} %get-tuple-element.4) | data formatting | bytes 2097152
  146.9 2.3 %copy.12 = bf16[128,4096]{1,0:T(8,128)(2,1)} copy(bf16[128,4096]{1,0:T(8,128)(2,1)} %get-tuple-element.5) | data formatting | bytes 2097152

commit v5 on v0

v5 whole, which is shorter than its diff:
```python
import jax
import jax.numpy as jnp
from jax import lax
from jax.experimental import pallas as pl
from jax.experimental.pallas import tpu as pltpu
from jax.sharding import PartitionSpec as P

BF = jnp.bfloat16
F32 = jnp.float32
RING = 4
PEERS = 16
SLOTS = 8
AXIAL = 6
DIAG = 9
ROWS = 72
MESH = pl.DeviceIdType.MESH


def flat_rows(block):
    return block.astype(F32).reshape(-1, block.shape[-1]).astype(BF)


def kernel(
    tokens, cotangent, ids_ref, probs_ref, wg, wu, wd,
    mixed_ref, grad_ref,
    tok, cot, perm, perm_back, slot_ref, prob_ref, one_d, wrow_d, wrow_g, coll_d, coll_g,
    sendg, sendd, x, wv, xs, xov, acc, accx, hid, rel, own_in, ret, retd, comb, combs, combr, fin,
    tk, g_s, g_r, d_s, d_r, ag_s, ag_r, rl_s, rl_r, wl, wx_s, wx_r,
    ac_s, ac_r, hd_s, hd_r, h_s, h_r, o_s, o_r, b_s, b_r, rd_s, rd_r, cs_s, cs_r,
    f_s, fy_r, fs_r, out_sem,
):
    e, t = lax.axis_index("expert"), lax.axis_index("tensor")
    ez, ex = e // RING, e % RING
    y, c = t // 2, t % 2
    right_y, left_y, far_y = (y + 1) % RING, (y + 3) % RING, (y + 2) % RING
    right, left, sib, far = right_y * 2 + c, left_y * 2 + c, y * 2 + 1 - c, far_y * 2 + c
    half = xs.shape[1] // 2
    core_width = half * RING

    def to_of(k):
        return ((ez + k // RING) % RING) * RING + (ex + k % RING) % RING

    def from_of(k):
        return ((ez + RING - k // RING) % RING) * RING + (ex + RING - k % RING) % RING

    def axial(j):
        return (1 + 2 * (j // 2) - 3 * (j // 4)) * (1 + 3 * (j % 2))

    def diag(j):
        place = (4 * j) % DIAG
        return (1 + place // 3) * RING + 1 + place % 3

    def remote(src, dst, ssem, rsem, pe, pt):
        return pltpu.make_async_remote_copy(
            src_ref=src, dst_ref=dst, send_sem=ssem, recv_sem=rsem,
            device_id={"expert": pe, "tensor": pt}, device_id_type=MESH,
        )

    def signal(pe, pt):
        pl.semaphore_signal(
            pltpu.get_barrier_semaphore(), inc=1,
            device_id={"expert": pe, "tensor": pt}, device_id_type=MESH,
        )

    mats = (wg, wu, wd)
    hu = wg.shape[1]

    def columns(core, v):
        return pl.ds(pl.multiple_of(core * core_width + v * half, half), half)

    def w_local(g, v):
        return pltpu.make_async_copy(
            mats[g].at[:, :, columns(c, v)], wv.at[g, v, :, pl.ds(0, hu), :], wl.at[0]
        )

    def w_cross(g, v):
        return remote(
            mats[g].at[:, :, columns(1 - c, v)], wv.at[g, v, :, pl.ds(128, hu), :],
            wx_s.at[0], wx_r.at[0], e, sib,
        )

    def taken(like, sem):
        pltpu.make_async_copy(like, like, sem).wait()

    def t_local(n, v):
        src, dst = ((tokens, tok), (cotangent, cot))[n]
        return pltpu.make_async_copy(src.at[:, columns(c, v)], dst.at[v], tk.at[n])

    for v in range(RING):
        for n in range(2):
            t_local(n, v).start()

    @pl.loop(1, PEERS)
    def _(k):
        signal(to_of(k), t)

    for other in (right, left, far, sib):
        signal(e, other)

    for g in range(3):
        for v in range(RING):
            w_local(g, v).start()

    count = ids_ref.shape[1]
    lane = lax.broadcasted_iota(jnp.int32, (count, count), 1)
    line = lax.broadcasted_iota(jnp.int32, (count, count), 0)
    chosen = jnp.zeros((count, count), F32)
    prob = jnp.zeros((count, count), F32)
    for k in range(ids_ref.shape[0]):
        match = ids_ref[k:k + 1, :] == line
        chosen = chosen + match.astype(F32)
        prob = prob + jnp.where(match, probs_ref[k:k + 1, :], 0.0)
    before = (line < lane).astype(F32).astype(BF)
    slot = jnp.dot(chosen.astype(BF), before, preferred_element_type=F32)
    slot_ref[...] = jnp.where(chosen > 0.5, slot, -1.0)
    prob_ref[...] = prob
    perm[...] = (lane == (line & 15) * SLOTS + (line >> 4)).astype(F32).astype(BF)
    perm_back[...] = (line == (lane & 15) * SLOTS + (lane >> 4)).astype(F32).astype(BF)

    def row_block(j):
        return pl.ds(pl.multiple_of(j * ROWS, SLOTS), ROWS)

    def build(d):
        block = pl.ds(pl.multiple_of(d * SLOTS, SLOTS), SLOTS)
        slots, weights = slot_ref[block, :], prob_ref[block, :]
        number = lax.broadcasted_iota(jnp.int32, (SLOTS, count), 0).astype(F32)
        place, weight = [], []
        for i in range(SLOTS):
            hit = slots[i:i + 1, :] == number
            place.append(hit.astype(F32))
            weight.append(jnp.where(hit, weights[i:i + 1, :], 0.0))
        hit = slots == float(SLOTS)
        place.append(hit.astype(F32))
        weight.append(jnp.where(hit, weights, 0.0))
        return jnp.concatenate(place, axis=0), jnp.concatenate(weight, axis=0)

    def fill(ref, one, weight, v):
        total = jnp.sum(weight, axis=1, keepdims=True)
        rows = jnp.dot(one, tok[v], preferred_element_type=F32)
        ref[:, :, 0:half] = rows.reshape(9, SLOTS, half).astype(BF)
        rows = jnp.dot(one, cot[v], preferred_element_type=F32) * total
        ref[:, :, half:] = rows.reshape(9, SLOTS, half).astype(BF)

    taken(tok, tk.at[0])
    taken(cot, tk.at[1])

    @pl.loop(0, DIAG)
    def _(j):
        place, weight = build(to_of(diag(j)))
        wrow_g[j // 3, row_block(j % 3), :] = weight
        fill(sendg.at[j], place.astype(BF), weight, y)

    @pl.loop(0, AXIAL)
    def _(j):
        place, weight = build(to_of(axial(j)))
        wrow_d[row_block(j), :] = weight
        one_d[j] = place.astype(BF)

    pl.semaphore_wait(pltpu.get_barrier_semaphore(), PEERS + 3)

    halves = (pl.ds(0, half), pl.ds(half, half))

    def slice_out(j, h):
        src, dst = sendg.at[j, :, :, halves[h]], x.at[y, :, e, :, halves[h]]
        return remote(src, dst, g_s.at[0], g_r.at[h, j], to_of(diag(j)), t)

    def slice_in(j, h):
        src, dst = sendg.at[j, :, :, halves[h]], x.at[y, :, from_of(diag(j)), :, halves[h]]
        return remote(src, dst, g_s.at[0], g_r.at[h, j], to_of(diag(j)), t)

    def whole_out(j, v, h):
        src, dst = sendd.at[v, j, :, :, halves[h]], x.at[v, :, e, :, halves[h]]
        return remote(src, dst, d_s.at[0], d_r.at[h, v], to_of(axial(j)), t)

    for h in range(2):
        @pl.loop(0, DIAG)
        def _(j, h=h):
            slice_out(j, h).start()

    for v in range(RING):
        for g in range(3):
            w_cross(g, v).start()

    def turn(q):
        return (y + RING + 2 * q - 1 - 3 * (q // 3) + (3 - q) // 3) % RING

    def start_whole(h):
        for q in range(RING):
            @pl.loop(0, AXIAL)
            def _(j, q=q):
                whole_out(j, turn(q), h).start()

    def pushed(n, j, h, dst_y, peer):
        s = from_of(diag(j))
        return remote(
            x.at[y, :, s, :, halves[h]], x.at[dst_y, :, s, :, halves[h]],
            ag_s.at[h], ag_r.at[h, j], e, peer,
        )

    def go_right(j, h):
        return pushed(0, j, h, y, right)

    def go_left(j, h):
        return pushed(1, j, h, y, left)

    def relay(j, h, slice_y, peer):
        ref = x.at[slice_y, :, from_of(diag(j)), :, halves[h]]
        return remote(ref, ref, rl_s.at[h], rl_r.at[h], e, peer)

    def relay_any(j, h):
        taken(own_in.at[:, j, :, :, halves[h]], ag_r.at[h, j])

        @pl.when((j + h) % 2 == 0)
        def _():
            relay(j, h, left_y, right).start()

        @pl.when((j + h) % 2 == 1)
        def _():
            relay(j, h, right_y, left).start()

    @pl.loop(0, DIAG)
    def _(j):
        slice_in(j, 0).wait_recv()
        go_right(j, 0).start()
        go_left(j, 0).start()

        @pl.when(j < DIAG - 1)
        def _():
            for u in range(3):
                n = 3 * j + u
                v, jj = turn(n // AXIAL), n % AXIAL
                fill(sendd.at[v, jj], one_d[jj], wrow_d[row_block(jj), :], v)

    start_whole(0)

    @pl.loop(0, DIAG)
    def _(j):
        relay_any(j, 0)

    @pl.loop(0, DIAG)
    def _(j):
        slice_in(j, 1).wait_recv()
        go_right(j, 1).start()
        go_left(j, 1).start()

    start_whole(1)
    place, weight = build(e)
    wrow_d[row_block(AXIAL), :] = weight
    place = place.astype(BF)
    for v in range(RING):
        fill(x.at[v, :, e], place, weight, v)

    zeros = jnp.zeros((8, 16, half), BF)
    for g in range(3):
        for v in range(RING):
            wv[g, v, :, hu:128, :] = zeros
            wv[g, v, :, 128 + hu:256, :] = zeros

    def split(ref, weights):
        weights = weights.T
        hi = weights.astype(BF)
        ref[0] = hi
        ref[1] = (weights - hi.astype(F32)).astype(BF)
        ref[2] = (weights > 0.0).astype(F32).astype(BF)

    wrow_d[(AXIAL + 1) * ROWS:, :] = jnp.zeros((wrow_d.shape[0] - (AXIAL + 1) * ROWS, count), F32)
    split(coll_d, wrow_d[...])
    for n in range(3):
        wrow_g[n, 3 * ROWS:, :] = jnp.zeros((wrow_g.shape[1] - 3 * ROWS, count), F32)
        split(coll_g.at[n], wrow_g[n])

    taken(wv.at[:, :, :, pl.ds(0, hu), :], wl.at[0])
    taken(wv.at[:, :, :, pl.ds(128, hu), :], wx_r.at[0])

    def acc_swap(i, h):
        group = pl.ds(2 * h, 2 - h)
        return remote(
            acc.at[group, i, :, pl.ds(128, 128)], accx.at[group, i], ac_s.at[0], ac_r.at[h, i],
            e, sib,
        )

    def hid_swap(i, h):
        group = pl.ds(h, 1 + h)
        return remote(
            hid.at[group, i, :, pl.ds(0, 128)], hid.at[group, i, :, pl.ds(128, 128)],
            hd_s.at[0], hd_r.at[h, i], e, sib,
        )

    def activate(i, h):
        acc_swap(i, h).wait_recv()
        if h == 0:
            pre = acc[0, i, :, 0:128] + accx[0, i]
            up = acc[1, i, :, 0:128] + accx[1, i]
            sg = jax.nn.sigmoid(pre)
            act = pre * sg
            hid[0, i, :, 0:128] = (act * up).astype(BF)
            acc[0, i, :, 0:128] = up * sg * (1.0 + pre * (1.0 - sg))
            acc[1, i, :, 0:128] = act
        else:
            gh = acc[2, i, :, 0:128] + accx[2, i]
            hid[1, i, :, 0:128] = (gh * acc[0, i, :, 0:128]).astype(BF)
            hid[2, i, :, 0:128] = (gh * acc[1, i, :, 0:128]).astype(BF)
        hid_swap(i, h).start()

    def contract(v, h, start=False, end=False):
        taken(sendd.at[v, :, :, :, halves[h]], d_r.at[h, v])

        over = flat_rows(x[v, 8, :, :, halves[h]])
        xov[:, halves[h]] = jnp.dot(perm[...], over, preferred_element_type=F32).astype(BF)

        @pl.loop(0, 8)
        def _(i):
            xs[0:128, halves[h]] = flat_rows(x[v, i, :, :, halves[h]])
            xs[128:144, halves[h]] = xov[pl.ds(pl.multiple_of(i * 16, 16), 16), halves[h]]
            for g in ((0, 1), (2,))[h]:
                part = lax.dot_general(
                    xs[:, halves[h]], wv[g, v, i], (((1,), (1,)), ((), ())),
                    preferred_element_type=F32,
                )
                if start:
                    acc[g, i] = part
                else:
                    acc[g, i] = acc[g, i] + part
            if end:
                acc_swap(i, h).start()

                @pl.when(i >= 2)
                def _():
                    activate(i - 2, h)

        if end:
            activate(6, h)
            activate(7, h)

    def relay_done(h):
        taken(rel.at[:, :, :, halves[h]], rl_r.at[h])

    def sent(h):
        taken(own_in.at[:, :, :, :, halves[h]], ag_s.at[h])
        taken(rel.at[:, :, :, halves[h]], rl_s.at[h])

    def relay_third(n):
        @pl.loop(3 * n, 3 * n + 3)
        def _(j):
            relay_any(j, 1)

    contract(y, 0, start=True)
    contract(right_y, 0)
    relay_third(0)
    contract(left_y, 0)
    relay_third(1)
    relay_done(0)
    contract(far_y, 0, end=True)
    relay_third(2)
    sent(0)

    def whole_back(j, v, h):
        src = x.at[v, :, from_of(axial(j)), :, halves[h]]
        return remote(
            src, retd.at[v, j, :, :, halves[h]], rd_s.at[0], rd_r.at[h, v],
            from_of(axial(j)), t,
        )

    def expand(v, h, start=False):
        @pl.loop(0, 8)
        def _(i):
            if start:
                hid_swap(i, h).wait_recv()
            if h == 0:
                out = jnp.dot(hid[0, i], wv[2, v, i], preferred_element_type=F32)
            else:
                out = jnp.dot(hid[1, i], wv[0, v, i], preferred_element_type=F32)
                out = out + jnp.dot(hid[2, i], wv[1, v, i], preferred_element_type=F32)
            x[v, i, :, :, halves[h]] = out[0:128].reshape(PEERS, SLOTS, half).astype(BF)
            tail = pl.ds(pl.multiple_of(i * 16, 16), 16)
            xov[tail, halves[h]] = out[128:144].astype(BF)

        over = jnp.dot(perm_back[...], xov[:, halves[h]], preferred_element_type=F32)
        x[v, 8, :, :, halves[h]] = over.reshape(PEERS, SLOTS, half).astype(BF)

    def return_whole(v, h):
        @pl.loop(0, AXIAL)
        def _(j):
            whole_back(j, v, h).start()

    def far_out(j, h, peer):
        src = x.at[far_y, :, from_of(diag(j)), :, halves[h]]
        return remote(src, rel.at[j, :, :, halves[h]], h_s.at[0], h_r.at[h, j], e, peer)

    def near(n, j, h, slice_y, peer):
        return remote(
            x.at[slice_y, :, from_of(diag(j)), :, halves[h]], own_in.at[n, j, :, :, halves[h]],
            o_s.at[0], o_r.at[h, j], e, peer,
        )

    def near_right(j, h):
        return near(0, j, h, right_y, right)

    def near_left(j, h):
        return near(1, j, h, left_y, left)

    def with_relayed(j, h, slice_y):
        far_out(j, h, right).wait_recv()
        s, cols = from_of(diag(j)), halves[h]
        total = x[slice_y, :, s, :, cols].astype(F32) + rel[j, :, :, cols].astype(F32)
        x[slice_y, :, s, :, cols] = total.astype(BF)

    def produce(h):
        expand(far_y, h, start=True)
        for j in range(DIAG):
            far_out(j, h, right if (j + h) % 2 == 0 else left).start()
        return_whole(far_y, h)
        expand(right_y, h)
        for j in range(1 - h, DIAG, 2):
            near_right(j, h).start()
        return_whole(right_y, h)
        expand(left_y, h)
        for j in range(h, DIAG, 2):
            near_left(j, h).start()
        return_whole(left_y, h)
        expand(y, h)
        return_whole(y, h)

    def add_relayed(h):
        @pl.loop(0, DIAG)
        def _(j):
            @pl.when((j + h) % 2 == 0)
            def _():
                with_relayed(j, h, right_y)
                near_right(j, h).start()

            @pl.when((j + h) % 2 == 1)
            def _():
                with_relayed(j, h, left_y)
                near_left(j, h).start()

    def gathered(coll, rows, h):
        width = rows.shape[0]
        if h == 1:
            return jnp.dot(coll[2, :, 0:width], rows, preferred_element_type=F32)
        part = jnp.dot(coll[0, :, 0:width], rows, preferred_element_type=F32)
        return part + jnp.dot(coll[1, :, 0:width], rows, preferred_element_type=F32)

    def whole_sum(v, h):
        retd[v, AXIAL, :, :, halves[h]] = x[v, :, e, :, halves[h]]

        taken(sendd.at[v, :, :, :, halves[h]], rd_r.at[h, v])

        return gathered(coll_d, flat_rows(retd[v, :, :, :, halves[h]]), h)

    def part_sum(n, h, peer):
        return remote(combs.at[h, n], combr.at[h, n], cs_s.at[0], cs_r.at[h], e, peer)

    def part_sums(h):
        for n, (v, peer) in enumerate(((far_y, far), (right_y, right), (left_y, left))):
            combs[h, n] = whole_sum(v, h).astype(BF)
            part_sum(n, h, peer).start()

    def slice_back(j, h):
        s = from_of(diag(j))
        return remote(
            x.at[y, :, s, :, halves[h]], ret.at[j, :, :, halves[h]], b_s.at[0], b_r.at[h, j // 3], s, t
        )

    def own_sums(h, first=0, last=DIAG):
        @pl.loop(first, last)
        def _(j):
            taken(own_in.at[:, j, :, :, halves[h]], o_r.at[h, j])
            s, cols = from_of(diag(j)), halves[h]
            total = x[y, :, s, :, cols].astype(F32) + own_in[0, j, :, :, cols].astype(F32)
            x[y, :, s, :, cols] = (total + own_in[1, j, :, :, cols].astype(F32)).astype(BF)
            slice_back(j, h).start()

    def finish(h):
        total = whole_sum(y, h)
        taken(combr.at[h], cs_r.at[h])
        for n in range(3):
            total = total + combr[h, n].astype(F32)
        comb[...] = total
        for n in range(3):
            taken(ret.at[pl.ds(3 * n, 3), :, :, halves[h]], b_r.at[h, n])
            rows = flat_rows(ret[3 * n:3 * n + 3, :, :, halves[h]])
            comb[...] = comb[...] + gathered(coll_g.at[n], rows, h)
        fin[t, :, halves[h]] = comb[...].astype(BF)

    rows_of = (pl.ds(0, 64), pl.ds(64, 64))
    def fin_y(n, h, slot_t, r, peer):
        ref = fin.at[slot_t, rows_of[r], halves[h]]
        return remote(ref, ref, f_s.at[0], fy_r.at[h, n], e, peer)

    def fin_s(n, h, slot_t, r):
        ref = fin.at[slot_t, rows_of[r], halves[h]]
        return remote(ref, ref, f_s.at[0], fs_r.at[h], e, sib)

    def push(copy):
        copy.start()

    def put(slot_t, owner_c, owner_y, h):
        ref = (mixed_ref, grad_ref)[h]
        pltpu.make_async_copy(
            fin.at[slot_t, :, halves[h]], ref.at[:, columns(owner_c, owner_y)], out_sem.at[h]
        ).start()

    def fin_start(h):
        push(fin_y(0, h, t, 0, right))
        push(fin_y(1, h, t, 1, left))
        push(fin_y(2, h, t, 1, right))
        push(fin_y(3, h, t, 0, left))
        push(fin_s(0, h, t, 0))
        push(fin_s(1, h, t, 1))

    def fin_relay(h):
        fin_y(0, h, left, 0, right).wait_recv()
        push(fin_y(4, h, left, 0, right))
        push(fin_s(2, h, left, 0))
        fin_y(1, h, right, 1, left).wait_recv()
        push(fin_y(5, h, right, 1, left))
        push(fin_s(3, h, right, 1))
        fin_y(2, h, left, 1, right).wait_recv()
        push(fin_s(4, h, left, 1))
        fin_y(3, h, right, 0, left).wait_recv()
        push(fin_s(5, h, right, 0))

    def fin_end(h):
        fin_y(4, h, far, 0, right).wait_recv()
        push(fin_s(6, h, far, 0))
        fin_y(5, h, far, 1, left).wait_recv()
        push(fin_s(7, h, far, 1))

    def fin_put(h):
        for owner_y in (y, left_y, right_y, far_y):
            put(owner_y * 2 + c, c, owner_y, h)
        taken(fin.at[pl.ds(0, RING), :, halves[h]], fs_r.at[h])
        for owner_y in (y, left_y, right_y, far_y):
            put(owner_y * 2 + 1 - c, 1 - c, owner_y, h)

    produce(0)
    contract(y, 1, start=True)
    contract(right_y, 1)
    add_relayed(0)
    contract(left_y, 1)
    relay_done(1)
    contract(far_y, 1, end=True)
    sent(1)
    produce(1)
    own_sums(0)
    part_sums(0)
    add_relayed(1)
    own_sums(1, 0, 6)
    part_sums(1)
    own_sums(1, 6)
    finish(0)
    fin_start(0)
    finish(1)
    fin_start(1)
    fin_relay(0)
    fin_relay(1)
    fin_end(0)
    fin_end(1)
    fin_put(0)
    fin_put(1)

    taken(sendg, g_s.at[0])
    taken(sendd, d_s.at[0])
    taken(wv.at[:, :, :, pl.ds(128, hu), :], wx_s.at[0])
    taken(accx, ac_s.at[0])
    taken(hid.at[:, :, :, pl.ds(0, 128)], hd_s.at[0])
    taken(rel, h_s.at[0])
    taken(own_in, o_s.at[0])
    taken(ret, b_s.at[0])
    taken(sendd, rd_s.at[0])
    taken(combs, cs_s.at[0])
    taken(fin.at[pl.ds(0, 2 * RING - 1)], f_s.at[0])
    taken(mixed_ref, out_sem.at[0])
    taken(grad_ref, out_sem.at[1])


def expert_kernel(tokens, cotangent, ids, probs, w_gate, w_up, w_down):
    tok, features = tokens.shape
    half = features // (2 * RING)
    width = 2 * half
    dma = pltpu.SemaphoreType.DMA
    vmem = pl.BlockSpec(memory_space=pltpu.VMEM)
    hbm = pl.BlockSpec(memory_space=pltpu.HBM)
    return pl.pallas_call(
        kernel,
        out_shape=[jax.ShapeDtypeStruct((tok, features), BF)] * 2,
        in_specs=[hbm] * 2 + [vmem] * 2 + [hbm] * 3,
        out_specs=[hbm] * 2,
        scratch_shapes=[
            pltpu.VMEM((RING, tok, half), BF),
            pltpu.VMEM((RING, tok, half), BF),
            pltpu.VMEM((tok, tok), BF),
            pltpu.VMEM((tok, tok), BF),
            pltpu.VMEM((tok, tok), F32),
            pltpu.VMEM((tok, tok), F32),
            pltpu.VMEM((AXIAL, ROWS, tok), BF),
            pltpu.VMEM((512, tok), F32),
            pltpu.VMEM((3, 256, tok), F32),
            pltpu.VMEM((3, tok, 512), BF),
            pltpu.VMEM((3, 3, tok, 256), BF),
            pltpu.VMEM((DIAG, 9, SLOTS, width), BF),
            pltpu.VMEM((RING, AXIAL, 9, SLOTS, width), BF),
            pltpu.VMEM((RING, 9, PEERS, SLOTS, width), BF),
            pltpu.VMEM((3, RING, 8, 256, half), BF),
            pltpu.VMEM((144, width), BF),
            pltpu.VMEM((128, width), BF),
            pltpu.VMEM((3, 8, 144, 256), F32),
            pltpu.VMEM((3, 8, 144, 128), F32),
            pltpu.VMEM((3, 8, 144, 256), BF),
            pltpu.VMEM((DIAG, 9, SLOTS, width), BF),
            pltpu.VMEM((2, DIAG, 9, SLOTS, width), BF),
            pltpu.VMEM((DIAG, 9, SLOTS, width), BF),
            pltpu.VMEM((RING, AXIAL + 1, 9, SLOTS, width), BF),
            pltpu.VMEM((tok, half), F32),
            pltpu.VMEM((2, 3, tok, half), BF),
            pltpu.VMEM((2, 3, tok, half), BF),
            pltpu.VMEM((2 * RING, tok, width), BF),
            dma((2,)),
            dma((1,)), dma((2, DIAG)),
            dma((1,)), dma((2, RING)),
            dma((2,)), dma((2, DIAG)),
            dma((2,)), dma((2,)),
            dma((1,)), dma((1,)), dma((1,)),
            dma((1,)), dma((2, 8)), dma((1,)), dma((2, 8)),
            dma((1,)), dma((2, DIAG)),
            dma((1,)), dma((2, DIAG)),
            dma((1,)), dma((2, 3)),
            dma((1,)), dma((2, RING)),
            dma((1,)), dma((2,)),
            dma((1,)), dma((2, 6)), dma((2,)),
            dma((2,)),
        ],
        compiler_params=pltpu.CompilerParams(
            collective_id=0, has_side_effects=True, vmem_limit_bytes=67_000_000
        ),
    )(tokens, cotangent, ids, probs, w_gate, w_up, w_down)


def body(tokens, cotangent, expert_ids, gate_probs, w_gate, w_up, w_down):
    return tuple(
        expert_kernel(
            tokens, cotangent, expert_ids.T, gate_probs.T, w_gate, w_up, w_down
        )
    )


def solution(mesh):
    return jax.shard_map(
        body,
        mesh=mesh,
        in_specs=(
            P("expert", None),
            P("expert", None),
            P("expert", None),
            P("expert", None),
            P("expert", "tensor", None),
            P("expert", "tensor", None),
            P("expert", "tensor", None),
        ),
        out_specs=(P("expert", None), P("expert", None)),
        check_vma=False,
    )
```

time: 610 us -> 135 us (0.22)
  waiting for transfers between devices: 226 us -> 0 us
  blocking collectives: 216 us -> 0 us
  Pallas kernels: 0 us -> 129 us
  matrix products: 87.9 us -> 0 us
  other arithmetic: 24.2 us -> 0 us
  local copies, waits for them, and re-layouts: 28.6 us -> 4.57 us
  between operations: 14.5 us -> 0.64 us
  starting transfers between devices: 6.79 us -> 0 us
    all_to_all x1 -> x0, blocking collectives: 216 us -> none  [body(): lax.all_to_all(buffer, 'expert', split_axis=0, concat_axis=0, tiled=True)]
    pallas_call x0 -> x1, Pallas kernels: none -> 129 us  [expert_kernel(): pl.pallas_call(kernel, out_shape=[jax.ShapeDtypeStruct((tok, features), B...]
    reduce_scatter x1 -> x0, waiting for transfers between devices: 100 us -> none  [body(): lax.psum_scatter(results.astype(jnp.bfloat16), 'tensor', scatter_dimensio...]
    dot_general x11 -> x0, matrix products: 87.9 us -> none  [the longest x1 15 us: expert_work(): jnp.einsum('sich,ihd->sicd', grad_up, w_up, preferred_element_type=jnp.fl...]
    psum x1 -> x0, waiting for transfers between devices: 66.4 us -> none  [body(): lax.psum(output_part.astype(jnp.bfloat16), 'tensor').astype(jnp.float32)]
    all_to_all x1 -> x0, waiting for transfers between devices: 59.8 us -> none  [body(): lax.all_to_all(reduced, 'expert', split_axis=0, concat_axis=0, tiled=True)]
    concatenate x1 -> x0, other arithmetic: 16.5 us -> none  [expert_work(): return jnp.concatenate([output_rows, grad_rows], axis=-1)]
    reshape x2 -> x0, local copies, waits for them, and re-layouts: 9.42 us -> none  [the longest x1 6.62 us: body(): buffer = buffer.reshape(expert_devs, local_experts, capacity, 2 * features)]
  transfers between devices with their start and end apart: 3 -> 0, of which waited for: 3 -> 0; matrix products, arithmetic and copies ran while one was open for 0% -> 0% of each run, Pallas kernels for 0% -> 0%
where the time goes in v5:
time: 135 us
  Pallas kernels  129 us (96%)
  local copies, waits for them, and re-layouts  4.57 us (3%)
    pallas_call x1, Pallas kernels, expert_kernel(): pl.pallas_call(kernel, out_shape=[jax.ShapeDtypeStruct((tok, features), B...  129 us
    unnamed x2, local copies, waits for them, and re-layouts  4.57 us

profile of v5, /device:TPU:1, one launch (start us, length us, event | category | flops | bytes accessed | tf_op | source)
XLA Modules:
  0.0 134.7 jit_solution(8683959551062818740)
XLA Ops:
  0.6 129.5 %shard_map.86 = (bf16[128,4096]{1,0:T(8,128)(2,1)}, bf16[128,4096]{1,0:T(8,128)(2,1)}) custom-call(bf16[128,4096]{1,0:T(8,128)(2,1)} %tokens.1, bf16[128,4096]{1,0:T(8,128)(2,1)} %cotangent.1, s32[8,128]{1,0:T(8,128)} %bitcast.2, f32[8,128]{1,0:T(8,128)} %bitcast.3, bf16[8,112,4096]{2,1,0:T(8,128)(2,1)} %wg.1, bf16[8,112,4096]{2,1,0:T(8,128)(2,1)} %wu.1, ...), custom_call_target="tpu_custom_call" | custom-call | tf_op jit(solution)/shard_map/pallas_call | solution.py:585
  130.1 2.3 %copy.11 = bf16[128,4096]{1,0:T(8,128)(2,1)} copy(bf16[128,4096]{1,0:T(8,128)(2,1)} %get-tuple-element.4) | data formatting | bytes 2097152
  132.4 2.3 %copy.12 = bf16[128,4096]{1,0:T(8,128)(2,1)} copy(bf16[128,4096]{1,0:T(8,128)(2,1)} %get-tuple-element.5) | data formatting | bytes 2097152

commit v6 on v5

--- a/solution.py
+++ b/solution.py
@@ -24,9 +24,9 @@
     tokens, cotangent, ids_ref, probs_ref, wg, wu, wd,
     mixed_ref, grad_ref,
     tok, cot, perm, perm_back, slot_ref, prob_ref, one_d, wrow_d, wrow_g, coll_d, coll_g,
-    sendg, sendd, x, wv, xs, xov, acc, accx, hid, rel, own_in, ret, retd, comb, combs, combr, fin,
+    sendg, sendd, x, wv, xs, xov, acc, accx, hid, rel, own_in, ret, retd, comb, combs, combr, combf, combh, fin,
     tk, g_s, g_r, d_s, d_r, ag_s, ag_r, rl_s, rl_r, wl, wx_s, wx_r,
-    ac_s, ac_r, hd_s, hd_r, h_s, h_r, o_s, o_r, b_s, b_r, rd_s, rd_r, cs_s, cs_r,
+    ac_s, ac_r, hd_s, hd_r, h_s, h_r, o_s, o_r, b_s, b_r, rd_s, rd_r, cs_s, cs_r, ch_s, ch_r,
     f_s, fy_r, fs_r, out_sem,
 ):
     e, t = lax.axis_index("expert"), lax.axis_index("tensor")
@@ -47,7 +47,7 @@
         return (1 + 2 * (j // 2) - 3 * (j // 4)) * (1 + 3 * (j % 2))
 
     def diag(j):
-        place = (4 * j) % DIAG
+        place = (7 * j) % DIAG
         return (1 + place // 3) * RING + 1 + place % 3
 
     def remote(src, dst, ssem, rsem, pe, pt):
@@ -94,7 +94,7 @@
     def _(k):
         signal(to_of(k), t)
 
-    for other in (right, left, far, sib):
+    for other in (right, left, sib):
         signal(e, other)
 
     for g in range(3):
@@ -156,7 +156,7 @@
         wrow_d[row_block(j), :] = weight
         one_d[j] = place.astype(BF)
 
-    pl.semaphore_wait(pltpu.get_barrier_semaphore(), PEERS + 3)
+    pl.semaphore_wait(pltpu.get_barrier_semaphore(), PEERS + 2)
 
     halves = (pl.ds(0, half), pl.ds(half, half))
 
@@ -451,10 +451,29 @@
     def part_sum(n, h, peer):
         return remote(combs.at[h, n], combr.at[h, n], cs_s.at[0], cs_r.at[h], e, peer)
 
-    def part_sums(h):
-        for n, (v, peer) in enumerate(((far_y, far), (right_y, right), (left_y, left))):
-            combs[h, n] = whole_sum(v, h).astype(BF)
-            part_sum(n, h, peer).start()
+    def part_half(n, h, peer):
+        return remote(combf.at[h, n], combh.at[h, n], ch_s.at[0], ch_r.at[h, n], e, peer)
+
+    quarter = half // 2
+
+    def far_sum(h):
+        total = whole_sum(far_y, h).astype(BF)
+        combf[h, 0] = total[:, 0:quarter]
+        combf[h, 1] = total[:, quarter:]
+        part_half(0, h, right).start()
+        part_half(1, h, left).start()
+
+    def near_sums(h):
+        total = whole_sum(right_y, h)
+        part_half(0, h, right).wait_recv()
+        combs[h, 0, :, 0:quarter] = (total[:, 0:quarter] + combh[h, 0].astype(F32)).astype(BF)
+        combs[h, 0, :, quarter:] = total[:, quarter:].astype(BF)
+        part_sum(0, h, right).start()
+        total = whole_sum(left_y, h)
+        part_half(1, h, left).wait_recv()
+        combs[h, 1, :, 0:quarter] = total[:, 0:quarter].astype(BF)
+        combs[h, 1, :, quarter:] = (total[:, quarter:] + combh[h, 1].astype(F32)).astype(BF)
+        part_sum(1, h, left).start()
 
     def slice_back(j, h):
         s = from_of(diag(j))
@@ -474,7 +493,7 @@
     def finish(h):
         total = whole_sum(y, h)
         taken(combr.at[h], cs_r.at[h])
-        for n in range(3):
+        for n in range(2):
             total = total + combr[h, n].astype(F32)
         comb[...] = total
         for n in range(3):
@@ -544,11 +563,13 @@
     sent(1)
     produce(1)
     own_sums(0)
-    part_sums(0)
+    far_sum(0)
     add_relayed(1)
     own_sums(1, 0, 6)
-    part_sums(1)
+    far_sum(1)
+    near_sums(0)
     own_sums(1, 6)
+    near_sums(1)
     finish(0)
     fin_start(0)
     finish(1)
@@ -570,6 +591,7 @@
     taken(ret, b_s.at[0])
     taken(sendd, rd_s.at[0])
     taken(combs, cs_s.at[0])
+    taken(combf, ch_s.at[0])
     taken(fin.at[pl.ds(0, 2 * RING - 1)], f_s.at[0])
     taken(mixed_ref, out_sem.at[0])
     taken(grad_ref, out_sem.at[1])
@@ -613,8 +635,10 @@
             pltpu.VMEM((DIAG, 9, SLOTS, width), BF),
             pltpu.VMEM((RING, AXIAL + 1, 9, SLOTS, width), BF),
             pltpu.VMEM((tok, half), F32),
-            pltpu.VMEM((2, 3, tok, half), BF),
-            pltpu.VMEM((2, 3, tok, half), BF),
+            pltpu.VMEM((2, 2, tok, half), BF),
+            pltpu.VMEM((2, 2, tok, half), BF),
+            pltpu.VMEM((2, 2, tok, half // 2), BF),
+            pltpu.VMEM((2, 2, tok, half // 2), BF),
             pltpu.VMEM((2 * RING, tok, width), BF),
             dma((2,)),
             dma((1,)), dma((2, DIAG)),
@@ -628,6 +652,7 @@
             dma((1,)), dma((2, 3)),
             dma((1,)), dma((2, RING)),
             dma((1,)), dma((2,)),
+            dma((1,)), dma((2, 2)),
             dma((1,)), dma((2, 6)), dma((2,)),
             dma((2,)),
         ],
@@ -637,12 +662,45 @@
     )(tokens, cotangent, ids, probs, w_gate, w_up, w_down)
 
 
+def copy_kernel(mixed_in, grad_in, mixed_ref, grad_ref, buf, in_sem, out_sem):
+    parts = buf.shape[1]
+    rows = buf.shape[2]
+    pairs = [
+        (n, p, src.at[pl.ds(p * rows, rows), :], dst.at[pl.ds(p * rows, rows), :])
+        for p in range(parts)
+        for n, (src, dst) in enumerate(((mixed_in, mixed_ref), (grad_in, grad_ref)))
+    ]
+    for n, p, src, _ in pairs:
+        pltpu.make_async_copy(src, buf.at[n, p], in_sem.at[n, p]).start()
+    for n, p, src, dst in pairs:
+        pltpu.make_async_copy(src, buf.at[n, p], in_sem.at[n, p]).wait()
+        pltpu.make_async_copy(buf.at[n, p], dst, out_sem.at[n, p]).start()
+    for n, p, _, dst in pairs:
+        pltpu.make_async_copy(buf.at[n, p], dst, out_sem.at[n, p]).wait()
+
+
+def copy_out(mixed, grad):
+    parts = 4
+    hbm = pl.BlockSpec(memory_space=pltpu.HBM)
+    rows, width = mixed.shape
+    return pl.pallas_call(
+        copy_kernel,
+        out_shape=[jax.ShapeDtypeStruct(mixed.shape, mixed.dtype)] * 2,
+        in_specs=[hbm] * 2,
+        out_specs=[hbm] * 2,
+        scratch_shapes=[
+            pltpu.VMEM((2, parts, rows // parts, width), mixed.dtype),
+            pltpu.SemaphoreType.DMA((2, parts)),
+            pltpu.SemaphoreType.DMA((2, parts)),
+        ],
+    )(mixed, grad)
+
+
 def body(tokens, cotangent, expert_ids, gate_probs, w_gate, w_up, w_down):
-    return tuple(
-        expert_kernel(
-            tokens, cotangent, expert_ids.T, gate_probs.T, w_gate, w_up, w_down
-        )
+    mixed, grad = expert_kernel(
+        tokens, cotangent, expert_ids.T, gate_probs.T, w_gate, w_up, w_down
     )
+    return tuple(copy_out(mixed, grad))
 
 
 def solution(mesh):

time: 135 us -> 129 us (0.956)
  local copies, waits for them, and re-layouts: 4.57 us -> 0 us
    unnamed x2 -> x0, local copies, waits for them, and re-layouts: 4.57 us -> none
    pallas_call x1, Pallas kernels: 129 us -> 126 us  [expert_kernel(): pl.pallas_call(kernel, out_shape=[jax.ShapeDtypeStruct((tok, features), B...]
    pallas_call x0 -> x1, Pallas kernels: none -> 2.39 us  [copy_out(): pl.pallas_call(copy_kernel, out_shape=[jax.ShapeDtypeStruct(mixed.shape,...]
where the time goes in v6:
time: 129 us
  Pallas kernels  129 us (100%)
    pallas_call x1, Pallas kernels, expert_kernel(): pl.pallas_call(kernel, out_shape=[jax.ShapeDtypeStruct((tok, features), B...  126 us

profile of v6, /device:TPU:1, one launch (start us, length us, event | category | flops | bytes accessed | tf_op | source)
XLA Modules:
  0.0 129.3 jit_solution(13001452669491918789)
XLA Ops:
  0.6 126.2 %shard_map.86 = (bf16[128,4096]{1,0:T(8,128)(2,1)}, bf16[128,4096]{1,0:T(8,128)(2,1)}) custom-call(bf16[128,4096]{1,0:T(8,128)(2,1)} %tokens.1, bf16[128,4096]{1,0:T(8,128)(2,1)} %cotangent.1, s32[8,128]{1,0:T(8,128)} %bitcast.2, f32[8,128]{1,0:T(8,128)} %bitcast.3, bf16[8,112,4096]{2,1,0:T(8,128)(2,1)} %wg.1, bf16[8,112,4096]{2,1,0:T(8,128)(2,1)} %wu.1, ...), custom_call_target="tpu_custom_call" | custom-call | tf_op jit(solution)/shard_map/pallas_call | solution.py:607
  126.9 2.4 %shard_map.87 = (bf16[128,4096]{1,0:T(8,128)(2,1)}, bf16[128,4096]{1,0:T(8,128)(2,1)}) custom-call(bf16[128,4096]{1,0:T(8,128)(2,1)} %get-tuple-element.4.mixed_in, bf16[128,4096]{1,0:T(8,128)(2,1)} %get-tuple-element.5.grad_in), custom_call_target="tpu_custom_call" | custom-call | tf_op jit(solution)/shard_map/pallas_call | solution.py:686
